TPU v7x, 128 devices: a whole 4x4x4 slice. The times are simulated.
128 devices in a mesh: layer: 8 (over y, core), lat: 16 (over x, z).
Axes of the slice: x: 4, y: 4, z: 4, core: 2. Of those that a mesh axis runs over, the one named last changes fastest.
Arguments:
- residuals: bfloat16 [8, 1024, 2048], P(None, ('layer', 'lat')), may hold values from -1100 to 1100
- topk_slots: int32 [8, 1024, 64], P(None, ('layer', 'lat')), may hold values from -1 to 65535, as said below
- dictionary: bfloat16 [8, 65536, 2048], P('layer', 'lat'), may hold values from -80 to 80
- enc_bias: float32 [8, 65536], P('layer', 'lat'), may hold values from 0.5 to 3
- dec_bias: float32 [8, 2048], P('layer'), may hold values from -5 to 5
- dead_ids: int32 [8, 256], P('layer'), may hold values from 0 to 65535, as said below
- seed_tokens: int32 [8, 256], P('layer'), may hold values from 0 to 1023
Outputs:
- reconstruction: bfloat16 [8, 1024, 2048], P(None, ('layer', 'lat'))
- unexplained: float32 [8], P('layer')
- latent_mass: float32 [8, 65536], P('layer', 'lat')
- new_rows: bfloat16 [8, 256, 2048], P('layer', 'lat')
- new_bias: float32 [8, 65536], P('layer', 'lat')
Inputs may be any that keep to these rules, and one draw needn't show every extreme that they name: `topk_slots`: slot s of a token belongs to latent shard s // 4: it holds -1 or an id from (s // 4) * 4096 to (s // 4 + 1) * 4096 - 1. Every token has exactly 32 slots that are not -1; ids may repeat. In every layer some token fills all 4 slots of one shard. `dead_ids`: the 256 ids of one layer are distinct.
All inputs are finite; a program needn't handle non-finite values.
Results may differ from a plain program's by a relative error of at most 0.009.
Values may be sent and summed in bfloat16 or wider, within the bound.
A program may use at most 128 MiB of HBM per device.

v0:
```python
import functools

import jax
import jax.numpy as jnp
from jax import lax
from jax.sharding import Mesh
from jax.sharding import PartitionSpec as P

LAT = ("lat_0", "lat_1")
LAYER = ("layer_0", "layer_1")
LAYER_LAT = ("layer_0", "layer_1", "lat_0", "lat_1")


def one_axis_at_a_time(shard, axes):
    return functools.reduce(lax.psum, axes, shard)


def split_up(shard, dim, size):
    before, after = (shard.shape[:dim], shard.shape[dim + 1 :])
    return jnp.moveaxis(shard.reshape(*before, size, -1, *after), dim, 0)


def joined_along(parts, dim):
    lengths = list(parts.shape[1:])
    lengths[dim] *= parts.shape[0]
    return jnp.moveaxis(parts, 0, dim).reshape(lengths)


def joined_exchange(shard, axis, axes, splits, concats):
    sizes = [lax.axis_size(a) for a in axes]
    parts = split_up(shard, splits[0], sizes[0])
    parts = jnp.moveaxis(split_up(parts, splits[1] + 1, sizes[1]), 0, 1)
    inside = parts.shape[2:]
    parts = parts.reshape(-1, *inside)
    parts = lax.all_to_all(parts, axis, split_axis=0, concat_axis=0, tiled=True)
    parts = joined_along(parts.reshape(*sizes, *inside), concats[0] + 1)
    return joined_along(parts, concats[1])


def token_position(global_tokens, tok_dev, lat_count, tok_group):
    blocks = global_tokens // tok_dev
    return blocks % lat_count * tok_group + blocks // lat_count * tok_dev + global_tokens % tok_dev


def body(residuals, topk_slots, dictionary, enc_bias, dec_bias, dead_ids, seed_tokens):
    layer_count = residuals.shape[0]
    tok_dev = residuals.shape[1]
    feature_width = residuals.shape[2]
    lat_count = lax.axis_size(LAT)
    layer_size = lax.axis_size(LAYER)
    shard_index = lax.axis_index(LAT)
    group_index = lax.axis_index(LAYER)
    lat_dev = dictionary.shape[1]
    tok_group = tok_dev * layer_size
    shard_rows = dictionary[0]
    row_norms = jnp.sqrt(jnp.sum(jnp.square(shard_rows.astype(jnp.float32)), axis=1) + 1e-06)
    norm_part = jnp.sum(row_norms)
    layer_slots = jnp.arange(layer_count, dtype=jnp.int32)
    norm_vector = jnp.where(layer_slots == group_index, norm_part, 0.0)
    squares = jnp.sum(jnp.square(residuals.astype(jnp.float32)), axis=(1, 2))
    totals, norm_totals = (
        one_axis_at_a_time(squares, LAYER_LAT),
        one_axis_at_a_time(norm_vector, LAYER_LAT),
    )
    norm_sum = lax.dynamic_index_in_dim(norm_totals, group_index, 0, keepdims=False)
    scales = lax.rsqrt(totals / (tok_dev * layer_size * lat_count * feature_width))
    outgoing = (residuals.astype(jnp.float32) * scales[:, None, None]).astype(jnp.bfloat16)
    regrouped = lax.all_to_all(outgoing, LAYER, split_axis=0, concat_axis=1, tiled=True)
    gathered = lax.all_gather(regrouped, LAT, axis=1, tiled=True)
    features = gathered[0]
    mine_slots = joined_exchange(topk_slots, LAYER_LAT, (LAYER, LAT), (0, 2), (1, 1))
    slot_major = mine_slots[0].T
    shifts = jnp.dot(
        shard_rows, dec_bias[0], precision=lax.Precision.HIGHEST, preferred_element_type=jnp.float32
    )
    is_live = slot_major >= 0
    clipped = jnp.where(is_live, slot_major - shard_index * lat_dev, 0)
    picked = jnp.take(shard_rows, clipped, axis=0)
    products = jnp.einsum("td,ctd->ct", features, picked, preferred_element_type=jnp.float32)
    picked_norms = row_norms[clipped]
    preact = (products - shifts[clipped]) / picked_norms + enc_bias[0][clipped]
    activity = jnp.where(is_live, jnp.maximum(preact, 0.0), 0.0)
    coefficient = (activity / picked_norms).astype(jnp.bfloat16)
    partial_value = jnp.einsum(
        "ct,ctd->td", coefficient, picked, preferred_element_type=jnp.float32
    )
    latent_mass = (
        jnp.zeros((lat_dev,), jnp.float32).at[clipped.reshape(-1)].add(activity.reshape(-1))
    )
    r_dev = seed_tokens.shape[1] // lat_count
    summed = lax.psum(partial_value.astype(jnp.bfloat16), LAT).astype(jnp.float32)
    estimate = summed + dec_bias[0]
    errors = features.astype(jnp.float32) - estimate
    numerator = jnp.sum(jnp.square(errors))
    estimate_own = lax.dynamic_slice_in_dim(estimate, shard_index * tok_group, tok_group, 0)
    my_seeds = lax.dynamic_slice_in_dim(seed_tokens[0], shard_index * r_dev, r_dev, 0)
    seeds = jnp.take(errors, token_position(my_seeds, tok_dev, lat_count, tok_group), axis=0)
    feat32 = features.astype(jnp.float32)
    centered = feat32 - jnp.mean(feat32, axis=0)
    denominator = jnp.sum(jnp.square(centered))
    unexplained = (numerator / denominator).reshape(1)
    seed_norm = jnp.sqrt(jnp.sum(jnp.square(seeds), axis=1, keepdims=True) + 1e-06)
    new_rows = (seeds / seed_norm * (norm_sum / (lat_dev * lat_count))).astype(jnp.bfloat16)[None]
    candidates = shard_index * lat_dev + jnp.arange(lat_dev, dtype=jnp.int32)
    is_dead = jnp.any(dead_ids[0][:, None] == candidates[None, :], axis=0)
    new_bias = jnp.where(is_dead, 0.0, enc_bias[0])[None]
    reconstruction = lax.all_to_all(
        estimate_own.astype(jnp.bfloat16)[None], LAYER, split_axis=1, concat_axis=0, tiled=True
    )
    return (reconstruction, unexplained, latent_mass[None], new_rows, new_bias)


def solution(mesh):
    split = Mesh(mesh.devices.reshape(4, 2, 4, 4), ("layer_0", "layer_1", "lat_0", "lat_1"))
    placed = (
        P(None, LAYER_LAT, None),
        P(None, LAYER_LAT, None),
        P(LAYER, LAT, None),
        P(LAYER, LAT),
        P(LAYER, None),
        P(LAYER, None),
        P(LAYER, None),
    )
    return jax.shard_map(
        body,
        mesh=split,
        in_specs=placed,
        out_specs=(
            P(None, LAYER_LAT, None),
            P(LAYER),
            P(LAYER, LAT),
            P(LAYER, LAT, None),
            P(LAYER, LAT),
        ),
        check_vma=False,
    )
```

profile of v0, /device:TPU:0, one launch (start us, length us, event | category | flops | bytes accessed | tf_op | source)
XLA Modules:
  0.0 438.9 jit_solution(7278936928870913223)
XLA Ops:
  7.2 0.0 all-gather.2.cloned.1.call-start
  7.2 0.0 copy-start.1
  7.2 0.0 copy-start.3
  7.2 7.2 %multiply_reduce_fusion = f32[4096]{0:T(1024)S(1)} fusion(bf16[1,4096,2048]{2,1,0:T(8,128)(2,1)} %param.9), kind=kLoop, calls=%fused_computation.6 | loop fusion | flops 25161728 | bytes 16793600 | tf_op jit(solution)/shard_map/reduce_sum | solution.py:56
  14.5 0.6 fusion.30
  15.1 0.2 fusion.7
  15.2 0.6 compare_select_fusion.4
  15.9 10.8 %all-reduce.2 = (f32[8]{0:T(128)S(1)}, f32[8]{0:T(128)S(1)}) all-reduce(f32[8]{0:T(128)S(1)} %fusion.7, f32[8]{0:T(128)S(1)} %compare_select_fusion.4), channel_id=1, replica_groups=mesh['layer_0'=4,'layer_1'=2,'lat_0'=4,'lat_1'=4] {'layer_0'}, use_global_device_ids=true, to_apply=%region_1.0 | all-reduce | flops 16 | bytes 128 | tf_op jit(solution)/shard_map/psum | solution.py:15
  26.7 2.4 all-reduce.3
  29.2 10.5 %all-reduce.1 = (f32[8]{0:T(128)S(1)}, f32[8]{0:T(128)S(1)}) all-reduce(f32[8]{0:T(128)S(1)} %get-tuple-element.11, f32[8]{0:T(128)S(1)} %get-tuple-element.12), channel_id=1, replica_groups=mesh['layer_0'=4,'layer_1'=2,'lat_0'=4,'lat_1'=4] {'lat_0'}, use_global_device_ids=true, to_apply=%region_3.4 | all-reduce | flops 16 | bytes 128 | tf_op jit(solution)/shard_map/psum | solution.py:15
  39.6 11.8 %all-reduce = (f32[8]{0:T(128)S(1)}, f32[8]{0:T(128)S(1)}) all-reduce(f32[8]{0:T(128)S(1)} %get-tuple-element.7, f32[8]{0:T(128)S(1)} %get-tuple-element.8), channel_id=1, replica_groups=mesh['layer_0'=4,'layer_1'=2,'lat_0'=4,'lat_1'=4] {'lat_1'}, use_global_device_ids=true, to_apply=%region_4.5 | all-reduce | flops 16 | bytes 128 | tf_op jit(solution)/shard_map/psum | solution.py:15
  51.4 0.1 fusion.8
  51.5 10.6 %all_to_all.29 = bf16[8,8,2048]{2,1,0:T(8,128)(2,1)} all-to-all(bf16[8,8,2048]{2,1,0:T(8,128)(2,1)S(1)} %fusion.8), channel_id=1, replica_groups=mesh['layer_0'=4,'layer_1'=2,'lat_0'=4,'lat_1'=4] {'layer_0','layer_1'}, dimensions={0} | all-to-all | bytes 524288 | tf_op jit(solution)/shard_map/all_to_all | solution.py:68
  62.1 0.0 all-gather.2.cloned.1.call-update
  62.1 0.0 copy-done.3
  62.2 0.1 copy.40
  62.3 0.8 copy.53
  63.1 4.6 %all-to-all-start = ((s32[128,1,8,4]{2,3,1,0:T(4,128)}), s32[128,1,8,4]{2,3,1,0:T(4,128)S(1)}, u32[]{:S(2)}, u32[]{:S(2)}) async-start(s32[128,1,8,4]{2,3,1,0:T(4,128)} %bitcast.2), calls=%async_computation | async-start | bytes 524288 | tf_op jit(solution)/shard_map/all_to_all | solution.py:35
  67.7 0.3 all-reduce.6.cloned.1.call-start
  68.1 16.6 %fusion.16 = f32[1,4096]{1,0:T(1,128)S(1)} fusion(f32[1,2048]{1,0:T(1,128)S(1)} %copy-done.2, bf16[1,4096,2048]{2,1,0:T(8,128)(2,1)} %param.9), kind=kOutput, calls=%fused_computation.49 | convolution fusion | flops 100663296 | bytes 16801792 | tf_op jit(solution)/shard_map/dot_general | solution.py:73
  84.6 0.0 all-to-all-done
  84.6 0.1 copy.43
  84.8 0.1 sub.45
  84.9 0.2 copy.46
  85.0 0.2 sub.47
  85.2 0.1 ge.30
  85.3 0.2 copy.44
  85.5 0.2 ge.32
  85.7 0.0 copy-start
  85.7 23.0 %gather_fusion.2 = f32[4096]{0:T(1024)S(1)} fusion(f32[4096]{0:T(1024)S(1)} %get-tuple-element.21, s32[4096]{0:T(1024)S(1)} %bitcast_clamp_fusion), kind=kCustom, calls=%fused_computation.2 | custom fusion | bytes 49152 | tf_op jit(solution)/shard_map/gather | solution.py:80
  108.8 0.0 copy-done
  108.8 23.0 %gather_fusion.3 = f32[4096]{0:T(1024)S(1)} fusion(f32[4096]{0:T(1024)S(1)} %bitcast.146, s32[4096]{0:T(1024)S(1)} %bitcast_clamp_fusion), kind=kCustom, calls=%fused_computation.3 | custom fusion | bytes 49152 | tf_op jit(solution)/shard_map/gather | solution.py:81
  131.9 23.0 %gather_fusion.1 = f32[4096]{0:T(1024)S(1)} fusion(f32[4096]{0:T(1024)S(1)} %bitcast.147, s32[4096]{0:T(1024)S(1)} %bitcast_clamp_fusion), kind=kCustom, calls=%fused_computation.1 | custom fusion | bytes 49152 | tf_op jit(solution)/shard_map/gather | solution.py:81
  154.9 39.3 %gather_fusion = bf16[4096,2048]{1,0:T(8,128)(2,1)} fusion(bf16[4096,2048]{1,0:T(8,128)(2,1)} %bitcast.148, s32[4096]{0:T(1024)S(1)} %bitcast_clamp_fusion), kind=kCustom, calls=%fused_computation | custom fusion | bytes 33570816 | tf_op jit(solution)/shard_map/jit(_take)/gather | solution.py:78
  194.2 14.1 %broadcast_select_fusion = bf16[4,1024,2048]{2,1,0:T(8,128)(2,1)} fusion(bf16[4,1024,2048]{2,1,0:T(8,128)(2,1)} %bitcast.149, pred[4,1024]{1,0:T(4,128)(4,1)S(1)} %compare_and_fusion), kind=kLoop, calls=%fused_computation.7 | loop fusion | flops 8388608 | bytes 33558528 | tf_op jit(solution)/shard_map/jit(_take)/select_n | solution.py:78
  208.3 46.0 %fusion.2 = f32[1024,1,4]{2,1,0:T(1,128)S(1)} fusion(bf16[4,1024,2048]{2,1,0:T(8,128)(2,1)} %broadcast_select_fusion, bf16[1024,2048,1]{1,0,2:T(8,128)(2,1)} %bitcast.150), kind=kOutput, calls=%fused_computation.10 | convolution fusion | flops 16777216 | bytes 20987904 | tf_op jit(solution)/shard_map/td,ctd->ct/dot_general | solution.py:79
  254.3 0.3 copy.50
  254.7 0.5 copy.51
  255.1 39.7 %fusion = bf16[1024,1,2048]{2,1,0:T(2,128)(2,1)S(1)} fusion(bf16[4,1024,1]{0,2,1:T(2,128)(2,1)S(1)} %copy.51, bf16[4,1024,2048]{2,1,0:T(8,128)(2,1)} %broadcast_select_fusion), kind=kOutput, calls=%fused_computation.8 | convolution fusion | flops 16777216 | bytes 20979712 | tf_op jit(solution)/shard_map/ct,ctd->td/dot_general | solution.py:84
  294.8 0.0 copy-start.5
  294.8 0.0 copy-start.4
  294.8 4.6 %copy.70 = bf16[1024,1,2048]{2,0,1:T(8,128)(2,1)} copy(bf16[1024,1,2048]{2,1,0:T(2,128)(2,1)S(1)} %fusion) | data formatting | bytes 8388608 | tf_op jit(solution)/shard_map/ct,ctd->td/dot_general | solution.py:84
  299.4 0.0 all-reduce.6.cloned.1.call-update
  299.4 0.6 dynamic_slice.18
  300.7 0.1 fusion.28
  300.8 0.1 compare_and_fusion.1
  300.9 0.6 compare_reduce_fusion
  301.5 0.6 reshape_select_fusion
  302.2 22.9 %scatter_custom_fusion = f32[4096]{0:T(1024)} fusion(s32[4096]{0:T(1024)S(1)} %bitcast.164, f32[4096]{0:T(1024)S(1)} %bitcast.165, f32[]{:T(128)} %constant.117.clone.1), kind=kCustom, calls=%fused_computation.51 | custom fusion | flops 4096 | bytes 16388 | tf_op jit(solution)/shard_map/scatter-add | solution.py:88
  325.1 2.9 convert_reduce_fusion
  328.0 76.2 %all-reduce.6.cloned.1.call-done = bf16[1024,2048]{1,0:T(8,128)(2,1)} async-done(((bf16[1024,2048]{1,0:T(8,128)(2,1)}), bf16[1024,2048]{1,0:T(8,128)(2,1)}) %all-reduce.6.cloned.1.call-update) | async-done | bytes 4194320 | tf_op jit(solution)/shard_map/psum | solution.py:91
  404.3 3.3 convert_add_fusion
  407.6 0.4 copy.73
  408.0 0.5 broadcast.403
  408.5 2.2 reduce
  410.7 1.0 reshape.394
  411.7 4.3 all-to-all-start.2
  416.0 7.3 %multiply_reduce_fusion.1 = (f32[]{:T(128)}, f32[1024,2048]{1,0:T(8,128)}, f32[]{:T(128)}) fusion(f32[2048]{0:T(1024)S(1)} %bitcast.160, bf16[1024,2048]{1,0:T(8,128)(2,1)} %all-reduce.6.cloned.1.call-done, bf16[1,1024,2048]{2,1,0:T(8,128)(2,1)} %all-gather.2.cloned.1.call-done, f32[2048]{0:T(1024)S(1)} %broadcast_multiply_fusion), kind=kLoop, calls=%fused_computation.18 | loop fusion | flops 18874366 | bytes 16793608 | tf_op jit(solution)/shard_map/reduce_sum | solution.py:94
  423.2 4.0 gather_fusion.4
  427.2 0.2 multiply_reduce_fusion.2
  428.8 0.7 fusion.12
  429.5 0.0 all-to-all-done.2
  429.5 0.3 reshape.395
  429.8 0.9 copy.71
  (24 shorter events, 0.2 us)
Async XLA Ops:
  7.2 201.1 %all-gather.2.cloned.1.call-start = ((), (), s32[]{:S(2)}) async-start(), calls=%async_computation.3 | async-start | bytes 4456448 | tf_op jit(solution)/shard_map/all_gather | solution.py:69
  7.2 7.9 %copy-start.1 = (bf16[8,8,2048]{2,1,0:T(8,128)(2,1)S(1)}, bf16[8,8,2048]{2,1,0:T(8,128)(2,1)}, u32[]{:S(2)}) copy-start(bf16[8,8,2048]{2,1,0:T(8,128)(2,1)} %param.7) | copy-start | bytes 786436
  7.2 54.9 %copy-start.3 = (s32[8,8,64]{2,1,0:T(8,128)S(1)}, s32[8,8,64]{2,1,0:T(8,128)}, u32[]{:S(2)}) copy-start(s32[8,8,64]{2,1,0:T(8,128)} %param.8) | copy-start | bytes 49156
  7.2 60.8 %copy-start.2 = (f32[1,2048]{1,0:T(1,128)S(1)}, f32[1,2048]{1,0:T(1,128)}, u32[]{:S(2)}) copy-start(f32[1,2048]{1,0:T(1,128)} %param.11) | copy-start | bytes 24580
  63.1 21.6 %all-to-all-start = ((s32[128,1,8,4]{2,3,1,0:T(4,128)}), s32[128,1,8,4]{2,3,1,0:T(4,128)S(1)}, u32[]{:S(2)}, u32[]{:S(2)}) async-start(s32[128,1,8,4]{2,3,1,0:T(4,128)} %bitcast.2), calls=%async_computation | async-start | bytes 524288 | tf_op jit(solution)/shard_map/all_to_all | solution.py:35
  67.7 336.5 %all-reduce.6.cloned.1.call-start = ((), (), s32[]{:S(2)}) async-start(), calls=%async_computation.4 | async-start | bytes 8388608 | tf_op jit(solution)/shard_map/psum | solution.py:91
  85.7 23.1 %copy-start = (f32[1,4096]{1,0:T(1,128)S(1)}, f32[1,4096]{1,0:T(1,128)}, u32[]{:S(2)}) copy-start(f32[1,4096]{1,0:T(1,128)} %param.10) | copy-start | bytes 49156
  294.8 5.9 %copy-start.5 = (s32[1,256]{1,0:T(1,128)S(1)}, s32[1,256]{1,0:T(1,128)}, u32[]{:S(2)}) copy-start(s32[1,256]{1,0:T(1,128)} %param.13) | copy-start | bytes 3076
  294.8 6.1 %copy-start.4 = (s32[1,256]{1,0:T(1,128)S(1)}, s32[1,256]{1,0:T(1,128)}, u32[]{:S(2)}) copy-start(s32[1,256]{1,0:T(1,128)} %param.12) | copy-start | bytes 3076
  411.7 17.9 %all-to-all-start.2 = ((bf16[8,2,8192]{2,1,0:T(2,128)(2,1)}), bf16[8,2,8192]{2,1,0:T(2,128)(2,1)S(1)}, u32[]{:S(2)}, u32[]{:S(2)}) async-start(bf16[8,2,8192]{2,1,0:T(2,128)(2,1)} %reshape.394), calls=%async_computation.2 | async-start | bytes 524288 | tf_op jit(solution)/shard_map/all_to_all | solution.py:107
Sparse Core Ops, SparseCore 0:
  62.3 48.7 all-gather.1
  299.5 104.6 all-reduce.5
where the time goes:
time: 443 us; the launch traced here: 439 us
  local copies, waits for them, and re-layouts  123 us (28%)
  matrix products  102 us (23%)
  waiting for transfers between devices  76.3 us (17%)
  other arithmetic  63.9 us (14%)
  blocking collectives  46.1 us (10%)
  between operations  17.7 us (4%)
  starting transfers between devices  9.27 us (2%)
    psum x1, waiting for transfers between devices, body(): lax.psum(partial_value.astype(jnp.bfloat16), LAT).astype(jnp.float32)  76.2 us
    gather x4, local copies, waits for them, and re-layouts, body(): preact = (products - shifts[clipped]) / picked_norms + enc_bias[0][clipped]  46.1 us
    dot_general x1, matrix products, body(): jnp.einsum('td,ctd->ct', features, picked, preferred_element_type=jnp.flo...  46 us
    dot_general x1, matrix products, body(): jnp.einsum('ct,ctd->td', coefficient, picked, preferred_element_type=jnp....  39.7 us
    gather x1, local copies, waits for them, and re-layouts, body(): picked = jnp.take(shard_rows, clipped, axis=0)  39.3 us
    psum x4, blocking collectives, one_axis_at_a_time(): return functools.reduce(lax.psum, axes, shard)  35.5 us
    gather x2, local copies, waits for them, and re-layouts, body(): picked_norms = row_norms[clipped]  23 us
    scatter-add x1, other arithmetic, body(): jnp.zeros((lat_dev,), jnp.float32).at[clipped.reshape(-1)]  22.9 us
  transfers between devices with their start and end apart: 4, of which 1 were waited for; matrix products, arithmetic and copies ran while one was open for 41% of the time, Pallas kernels for 0%

commit v1 on v0

v1 whole, which is shorter than its diff:
```python
import functools

import jax
import jax.numpy as jnp
from jax import lax
from jax.experimental import pallas as pl
from jax.experimental.pallas import tpu as pltpu
from jax.sharding import Mesh
from jax.sharding import PartitionSpec as P

LAT = ("lat_0", "lat_1")
LAYER = ("layer_0", "layer_1")
LAYER_LAT = ("layer_0", "layer_1", "lat_0", "lat_1")
TILE = 512
BLOCK = 256


def split_up(shard, dim, size):
    before, after = (shard.shape[:dim], shard.shape[dim + 1 :])
    return jnp.moveaxis(shard.reshape(*before, size, -1, *after), dim, 0)


def joined_along(parts, dim):
    lengths = list(parts.shape[1:])
    lengths[dim] *= parts.shape[0]
    return jnp.moveaxis(parts, 0, dim).reshape(lengths)


def joined_exchange(shard, axis, axes, splits, concats):
    sizes = [lax.axis_size(a) for a in axes]
    parts = split_up(shard, splits[0], sizes[0])
    parts = jnp.moveaxis(split_up(parts, splits[1] + 1, sizes[1]), 0, 1)
    inside = parts.shape[2:]
    parts = parts.reshape(-1, *inside)
    parts = lax.all_to_all(parts, axis, split_axis=0, concat_axis=0, tiled=True)
    parts = joined_along(parts.reshape(*sizes, *inside), concats[0] + 1)
    return joined_along(parts, concats[1])


def token_position(global_tokens, tok_dev, lat_count, tok_group):
    blocks = global_tokens // tok_dev
    return blocks % lat_count * tok_group + blocks // lat_count * tok_dev + global_tokens % tok_dev


def row_stats(w, dec, shift, inv, norm, j):
    d = w.shape[1]
    sq = dc = None
    for g in range(d // 128):
        piece = w[pl.ds(j * TILE, TILE), g * 128 : (g + 1) * 128].astype(jnp.float32)
        a, b = piece * piece, piece * dec[0:1, g * 128 : (g + 1) * 128]
        sq, dc = (a, b) if sq is None else (sq + a, dc + b)
    ones = jnp.ones((8, 128), jnp.float32)
    dims = (((1,), (1,)), ((), ()))
    hi = lax.Precision.HIGHEST
    total = lax.dot_general(ones, sq, dims, precision=hi, preferred_element_type=jnp.float32)
    n = jnp.sqrt(total + 1e-06)
    norm[j] = n
    inv[j] = 1.0 / n
    shift[j] = lax.dot_general(ones, dc, dims, precision=hi, preferred_element_type=jnp.float32)


def encode_tile(feats, w, slot, shift, inv, enc, mass, coef, j):
    wt = w[pl.ds(j * TILE, TILE), :]
    p = lax.dot_general(feats[...], wt, (((1,), (1,)), ((), ())), preferred_element_type=jnp.float32)
    rows = p.shape[0]
    p = p.reshape(rows // 8, 8, TILE)
    act = jnp.maximum((p - shift[j]) * inv[j] + enc[j], 0.0)
    kept = []
    for g in range(TILE // 128):
        a = act[:, :, g * 128 : (g + 1) * 128]
        base = (j * TILE + g * 128).astype(jnp.float32)
        total = None
        for c in range(4):
            hit = jnp.where(slot[c] == base, a, 0.0)
            total = hit if total is None else total + hit
        kept.append(total)
    kept = jnp.concatenate(kept, axis=2)
    mass[j] += jnp.sum(kept, axis=0)
    at = pl.ds(pl.multiple_of(j * TILE, TILE), TILE)
    coef[:, at] = (kept * inv[j]).reshape(rows, TILE).astype(jnp.bfloat16)


def dense_kernel(feats, w, dec, enc, slots, part, mass, norm, shift, inv, slot, coef):
    tiles = w.shape[0] // TILE

    @pl.when(pl.program_id(0) == 0)
    def _():
        mass[...] = jnp.zeros_like(mass)
        lax.fori_loop(0, tiles, lambda j, _: row_stats(w, dec, shift, inv, norm, j), None)

    lanes = lax.broadcasted_iota(jnp.int32, (BLOCK, 128), 1)
    for c in range(4):
        delta = slots[:, c : c + 1] - lanes
        slot[c] = delta.astype(jnp.float32).reshape(BLOCK // 8, 8, 128)

    lax.fori_loop(
        0, tiles, lambda j, _: encode_tile(feats, w, slot, shift, inv, enc, mass, coef, j), None
    )

    @pl.loop(0, w.shape[1] // TILE)
    def _(n):
        at = pl.ds(pl.multiple_of(n * TILE, TILE), TILE)
        part[:, at] = jnp.dot(coef[...], w[:, at], preferred_element_type=jnp.float32).astype(jnp.bfloat16)


def dense(features, rows, dec, enc, slots):
    tokens, d = features.shape
    lats = rows.shape[0]
    tiles = lats // TILE
    whole = lambda *shape: pl.BlockSpec(
        shape, lambda b: (0,) * len(shape), pipeline_mode=pl.Buffered(1)
    )
    stat = (tiles, 8, TILE)
    enc8 = jnp.broadcast_to(enc.reshape(tiles, 1, TILE), stat)
    return pl.pallas_call(
        dense_kernel,
        out_shape=(
            jax.ShapeDtypeStruct((tokens, d), jnp.bfloat16),
            jax.ShapeDtypeStruct(stat, jnp.float32),
            jax.ShapeDtypeStruct(stat, jnp.float32),
        ),
        grid=(tokens // BLOCK,),
        in_specs=[
            pl.BlockSpec((BLOCK, d), lambda b: (b, 0)),
            whole(lats, d),
            whole(1, d),
            whole(*stat),
            pl.BlockSpec((BLOCK, 4), lambda b: (b, 0)),
        ],
        out_specs=(pl.BlockSpec((BLOCK, d), lambda b: (b, 0)), whole(*stat), whole(*stat)),
        scratch_shapes=[
            pltpu.VMEM(stat, jnp.float32),
            pltpu.VMEM(stat, jnp.float32),
            pltpu.VMEM((4, BLOCK // 8, 8, 128), jnp.float32),
            pltpu.VMEM((BLOCK, lats), jnp.bfloat16),
        ],
        compiler_params=pltpu.CompilerParams(vmem_limit_bytes=56 * 2**20),
        name="dense",
    )(features, rows, dec, enc8, slots)


def body(residuals, topk_slots, dictionary, enc_bias, dec_bias, dead_ids, seed_tokens):
    tok_dev = residuals.shape[1]
    lat_count = lax.axis_size(LAT)
    layer_size = lax.axis_size(LAYER)
    shard_index = lax.axis_index(LAT)
    lat_dev = dictionary.shape[1]
    tok_group = tok_dev * layer_size
    regrouped = lax.all_to_all(residuals, LAYER, split_axis=0, concat_axis=1, tiled=True)
    gathered = lax.all_gather(regrouped, LAT, axis=1, tiled=True)[0]
    mine_slots = joined_exchange(topk_slots, LAYER_LAT, (LAYER, LAT), (0, 2), (1, 1))[0]
    wide = gathered.astype(jnp.float32)
    scale = lax.rsqrt(jnp.mean(jnp.square(wide)))
    features = (wide * scale).astype(jnp.bfloat16)
    local_slots = jnp.where(mine_slots >= 0, mine_slots - shard_index * lat_dev, -(2**16))
    partial_value, mass8, norm8 = dense(
        features, dictionary[0], dec_bias, enc_bias[0], local_slots
    )
    latent_mass = jnp.sum(mass8, axis=1).reshape(1, lat_dev)
    norm_sum = lax.psum(jnp.sum(norm8[:, 0, :]), LAT)
    r_dev = seed_tokens.shape[1] // lat_count
    summed = lax.psum(partial_value, LAT).astype(jnp.float32)
    estimate = summed + dec_bias[0]
    errors = features.astype(jnp.float32) - estimate
    numerator = jnp.sum(jnp.square(errors))
    estimate_own = lax.dynamic_slice_in_dim(estimate, shard_index * tok_group, tok_group, 0)
    my_seeds = lax.dynamic_slice_in_dim(seed_tokens[0], shard_index * r_dev, r_dev, 0)
    seeds = jnp.take(errors, token_position(my_seeds, tok_dev, lat_count, tok_group), axis=0)
    feat32 = features.astype(jnp.float32)
    centered = feat32 - jnp.mean(feat32, axis=0)
    denominator = jnp.sum(jnp.square(centered))
    unexplained = (numerator / denominator).reshape(1)
    seed_norm = jnp.sqrt(jnp.sum(jnp.square(seeds), axis=1, keepdims=True) + 1e-06)
    new_rows = (seeds / seed_norm * (norm_sum / (lat_dev * lat_count))).astype(jnp.bfloat16)[None]
    candidates = shard_index * lat_dev + jnp.arange(lat_dev, dtype=jnp.int32)
    is_dead = jnp.any(dead_ids[0][:, None] == candidates[None, :], axis=0)
    new_bias = jnp.where(is_dead, 0.0, enc_bias[0])[None]
    reconstruction = lax.all_to_all(
        estimate_own.astype(jnp.bfloat16)[None], LAYER, split_axis=1, concat_axis=0, tiled=True
    )
    return (reconstruction, unexplained, latent_mass, new_rows, new_bias)


def solution(mesh):
    split = Mesh(mesh.devices.reshape(4, 2, 4, 4), ("layer_0", "layer_1", "lat_0", "lat_1"))
    placed = (
        P(None, LAYER_LAT, None),
        P(None, LAYER_LAT, None),
        P(LAYER, LAT, None),
        P(LAYER, LAT),
        P(LAYER, None),
        P(LAYER, None),
        P(LAYER, None),
    )
    return jax.shard_map(
        body,
        mesh=split,
        in_specs=placed,
        out_specs=(
            P(None, LAYER_LAT, None),
            P(LAYER),
            P(LAYER, LAT),
            P(LAYER, LAT, None),
            P(LAYER, LAT),
        ),
        check_vma=False,
    )
```

time: 443 us -> 299 us (0.67)
  local copies, waits for them, and re-layouts: 123 us -> 12.1 us
  matrix products: 102 us -> 0 us
  Pallas kernels: 0 us -> 68.7 us
  other arithmetic: 63.9 us -> 30.4 us
  waiting for transfers between devices: 76.3 us -> 103 us
  blocking collectives: 46.1 us -> 52.1 us
    gather x7 -> x0, local copies, waits for them, and re-layouts: 108 us -> none  [the longest x4 46.1 us: body(): preact = (products - shifts[clipped]) / picked_norms + enc_bias[0][clipped]]
    dot_general x3 -> x0, matrix products: 102 us -> none  [the longest x1 46 us: body(): jnp.einsum('td,ctd->ct', features, picked, preferred_element_type=jnp.flo...]
    pallas_call x0 -> x1, Pallas kernels: none -> 68.7 us  [dense(): pl.pallas_call(dense_kernel, out_shape=(jax.ShapeDtypeStruct((tokens, d),...]
    all_gather x1, waiting for transfers between devices: 0.01 us -> 29.1 us  [body(): gathered = lax.all_gather(regrouped, LAT, axis=1, tiled=True)[0]]
    scatter-add x1 -> x0, other arithmetic: 22.9 us -> none  [body(): jnp.zeros((lat_dev,), jnp.float32).at[clipped.reshape(-1)]]
    psum x1, waiting for transfers between devices: 76.2 us -> 59.9 us  [body(): summed = lax.psum(partial_value, LAT).astype(jnp.float32)]
    select_n x3 -> x1, other arithmetic: 14.8 us -> 0.07 us  [body(): jnp.where(mine_slots >= 0, mine_slots - shard_index * lat_dev, -2 ** 16)]
    all_to_all x1, waiting for transfers between devices: 0.01 us -> 8.84 us  [joined_exchange(): parts = lax.all_to_all(parts, axis, split_axis=0, concat_axis=0, tiled=True)]
  transfers between devices with their start and end apart: 4 -> 4, of which waited for: 1 -> 4; matrix products, arithmetic and copies ran while one was open for 41% -> 4% of each run, Pallas kernels for 0% -> 0%
where the time goes in v1:
time: 299 us; the launch traced here: 298 us
  waiting for transfers between devices  103 us (34%)
  Pallas kernels  68.7 us (23%)
  blocking collectives  52.1 us (17%)
  other arithmetic  30.4 us (10%)
  between operations  17.9 us (6%)
  starting transfers between devices  13.4 us (4%)
  local copies, waits for them, and re-layouts  12.1 us (4%)
    pallas_call x1, Pallas kernels, dense(): pl.pallas_call(dense_kernel, out_shape=(jax.ShapeDtypeStruct((tokens, d),...  68.7 us
    psum x1, waiting for transfers between devices, body(): summed = lax.psum(partial_value, LAT).astype(jnp.float32)  59.9 us
    psum x1, blocking collectives, body(): norm_sum = lax.psum(jnp.sum(norm8[:, 0, :]), LAT)  39.9 us
    all_gather x1, waiting for transfers between devices, body(): gathered = lax.all_gather(regrouped, LAT, axis=1, tiled=True)[0]  29.1 us
    all_to_all x1, blocking collectives, body(): lax.all_to_all(residuals, LAYER, split_axis=0, concat_axis=1, tiled=True)  12.2 us
    all_to_all x1, starting transfers between devices, joined_exchange(): parts = lax.all_to_all(parts, axis, split_axis=0, concat_axis=0, tiled=True)  9.03 us
    all_to_all x1, waiting for transfers between devices, joined_exchange(): parts = lax.all_to_all(parts, axis, split_axis=0, concat_axis=0, tiled=True)  8.84 us
    reduce_sum x1, other arithmetic, body(): numerator = jnp.sum(jnp.square(errors))  7.25 us
  transfers between devices with their start and end apart: 4, of which 4 were waited for; matrix products, arithmetic and copies ran while one was open for 4% of the time, Pallas kernels for 0%

profile of v1, /device:TPU:0, one launch (start us, length us, event | category | flops | bytes accessed | tf_op | source)
XLA Modules:
  0.0 297.9 jit_solution(18263931080219019157)
XLA Ops:
  7.2 0.0 all-gather.2.cloned.1.call-start
  7.2 12.2 %all_to_all.29 = bf16[8,8,2048]{2,1,0:T(8,128)(2,1)} all-to-all(bf16[8,8,2048]{2,1,0:T(8,128)(2,1)} %param.7), channel_id=1, replica_groups=mesh['layer_0'=4,'layer_1'=2,'lat_0'=4,'lat_1'=4] {'layer_0','layer_1'}, dimensions={0} | all-to-all | bytes 524288 | tf_op jit(solution)/shard_map/all_to_all | solution.py:149
  19.4 0.0 all-gather.2.cloned.1.call-update
  19.4 0.9 copy.27
  20.4 0.8 copy.33
  21.1 9.0 %all-to-all-start.1 = ((s32[128,1,8,4]{2,3,1,0:T(4,128)}), s32[128,1,8,4]{2,3,1,0:T(4,128)S(1)}, u32[]{:S(2)}, u32[]{:S(2)}) async-start(s32[128,1,8,4]{2,3,1,0:T(4,128)} %bitcast.5), calls=%async_computation.1 | async-start | bytes 524288 | tf_op jit(solution)/shard_map/all_to_all | solution.py:35
  30.2 0.0 all-reduce.2.cloned.1.call-start
  30.2 1.3 compare_reduce_fusion
  31.5 0.5 broadcast.360
  32.0 2.0 reshape_select_fusion
  34.0 8.8 %all-to-all-done.1 = s32[128,1,8,4]{2,3,1,0:T(4,128)S(1)} async-done(((s32[128,1,8,4]{2,3,1,0:T(4,128)}), s32[128,1,8,4]{2,3,1,0:T(4,128)S(1)}, u32[]{:S(2)}, u32[]{:S(2)}) %all-to-all-start.1) | async-done | bytes 16416 | tf_op jit(solution)/shard_map/all_to_all | solution.py:35
  42.9 0.1 subtract_select_fusion
  43.0 0.1 copy.34
  43.1 1.3 copy.31
  44.4 29.1 %all-gather.2.cloned.1.call-done = bf16[1,1024,2048]{2,1,0:T(8,128)(2,1)} async-done(((bf16[1,64,2048]{2,1,0:T(8,128)(2,1)}), bf16[1,1024,2048]{2,1,0:T(8,128)(2,1)}) %all-gather.2.cloned.1.call-update) | async-done | bytes 4194320 | tf_op jit(solution)/shard_map/all_gather | solution.py:150
  73.6 4.9 %fusion = f32[]{:T(128)} fusion(bf16[1,1024,2048]{2,1,0:T(8,128)(2,1)} %all-gather.2.cloned.1.call-done), kind=kLoop, calls=%fused_computation.6 | loop fusion | flops 6291455 | bytes 4194308 | tf_op jit(solution)/shard_map/reduce_sum | solution.py:153
  79.2 5.7 %convert_reduce_fusion = (f32[2048]{0:T(1024)S(1)}, bf16[1024,2048]{1,0:T(8,128)(2,1)}) fusion(f32[]{:T(128)S(6)} %rsqrt.3, bf16[1,1024,2048]{2,1,0:T(8,128)(2,1)} %all-gather.2.cloned.1.call-done), kind=kLoop, calls=%fused_computation.2 | loop fusion | flops 10483712 | bytes 8396804 | tf_op jit(solution)/shard_map/reduce_sum | solution.py:170
  84.9 0.7 broadcast_in_dim.38.enc
  85.6 0.0 copy-start.1
  85.6 0.0 copy-start
  85.6 68.7 %dense.1 = (bf16[1024,2048]{1,0:T(8,128)(2,1)}, f32[8,8,512]{2,1,0:T(8,128)}, f32[8,8,512]{2,1,0:T(8,128)}) custom-call(bf16[1024,2048]{1,0:T(8,128)(2,1)} %get-tuple-element.12.feats, bf16[4096,2048]{1,0:T(8,128)(2,1)} %bitcast.67, f32[1,2048]{1,0:T(1,128)} %dec.1, f32[8,8,512]{2,1,0:T(8,128)} %broadcast_in_dim.38.enc, s32[1024,4]{1,0:T(8,128)} %bitcast.68), custom_call_target="tpu_custom_call" | custom-call | tf_op jit(solution)/shard_map/dense/pallas_call | solution.py:115
  154.3 0.0 all-reduce.2.cloned.1.call-update
  154.3 0.0 copy-done.1
  154.3 0.1 compare_and_fusion
  154.5 0.1 fusion.15
  154.6 1.5 slice_reduce_fusion
  156.1 39.9 %psum.15 = f32[]{:T(128)} all-reduce(f32[]{:T(128)} %slice_reduce_fusion), channel_id=1, replica_groups=mesh['layer_0'=4,'layer_1'=2,'lat_0'=4,'lat_1'=4] {'lat_0','lat_1'}, use_global_device_ids=true, to_apply=%region_8.9 | all-reduce | flops 1 | bytes 8 | tf_op jit(solution)/shard_map/psum | solution.py:160
  196.0 0.9 reduce_sum.67
  196.9 0.6 copy.37
  198.2 59.9 %all-reduce.2.cloned.1.call-done = bf16[1024,2048]{1,0:T(8,128)(2,1)} async-done(((bf16[1024,2048]{1,0:T(8,128)(2,1)}), bf16[1024,2048]{1,0:T(8,128)(2,1)}) %all-reduce.2.cloned.1.call-update) | async-done | bytes 4194320 | tf_op jit(solution)/shard_map/psum | solution.py:162
  258.1 0.0 copy-done
  258.1 7.3 %multiply_reduce_fusion = (f32[]{:T(128)}, f32[1024,2048]{1,0:T(8,128)}, f32[]{:T(128)}) fusion(f32[2048]{0:T(1024)S(1)} %bitcast.76, bf16[1024,2048]{1,0:T(8,128)(2,1)} %all-reduce.2.cloned.1.call-done, bf16[1024,2048]{1,0:T(8,128)(2,1)} %get-tuple-element.12.feats, f32[2048]{0:T(1024)S(1)} %broadcast_multiply_fusion), kind=kLoop, calls=%fused_computation.10 | loop fusion | flops 18874366 | bytes 16793608 | tf_op jit(solution)/shard_map/reduce_sum | solution.py:165
  265.3 4.0 %gather_fusion = f32[16,2048]{1,0:T(8,128)S(1)} fusion(f32[1024,2048]{1,0:T(8,128)} %get-tuple-element.14, s32[1024]{0:T(1024)S(1)} %pad_clamp_fusion), kind=kCustom, calls=%fused_computation | custom fusion | bytes 262208 | tf_op jit(solution)/shard_map/jit(_take)/gather | solution.py:168
  269.4 0.2 multiply_reduce_fusion.1
  269.6 3.3 %convert_add_fusion = bf16[1024,2048]{1,0:T(8,128)(2,1)S(1)} fusion(bf16[1024,2048]{1,0:T(8,128)(2,1)} %all-reduce.2.cloned.1.call-done, f32[2048]{0:T(1024)S(1)} %bitcast.77), kind=kLoop, calls=%fused_computation.11 | loop fusion | flops 6291456 | bytes 8396800 | tf_op jit(solution)/shard_map/add | solution.py:163
  272.9 0.4 copy.41
  273.3 0.5 broadcast.361
  273.9 2.2 reduce.7
  276.0 1.0 reshape.317
  277.0 4.3 %all-to-all-start.2 = ((bf16[8,2,8192]{2,1,0:T(2,128)(2,1)}), bf16[8,2,8192]{2,1,0:T(2,128)(2,1)S(1)}, u32[]{:S(2)}, u32[]{:S(2)}) async-start(bf16[8,2,8192]{2,1,0:T(2,128)(2,1)} %reshape.317), calls=%async_computation.2 | async-start | bytes 524288 | tf_op jit(solution)/shard_map/all_to_all | solution.py:178
  282.6 0.7 fusion.8
  283.3 5.6 %all-to-all-done.2 = bf16[8,2,8192]{2,1,0:T(2,128)(2,1)S(1)} async-done(((bf16[8,2,8192]{2,1,0:T(2,128)(2,1)}), bf16[8,2,8192]{2,1,0:T(2,128)(2,1)S(1)}, u32[]{:S(2)}, u32[]{:S(2)}) %all-to-all-start.2) | async-done | bytes 262176 | tf_op jit(solution)/shard_map/all_to_all | solution.py:178
  288.8 0.3 reshape.318
  289.1 0.9 copy.40
  (6 shorter events, 0.1 us)
Async XLA Ops:
  7.2 66.4 %all-gather.2.cloned.1.call-start = ((), (), s32[]{:S(2)}) async-start(), calls=%async_computation.3 | async-start | bytes 4456448 | tf_op jit(solution)/shard_map/all_gather | solution.py:150
  21.1 21.8 %all-to-all-start.1 = ((s32[128,1,8,4]{2,3,1,0:T(4,128)}), s32[128,1,8,4]{2,3,1,0:T(4,128)S(1)}, u32[]{:S(2)}, u32[]{:S(2)}) async-start(s32[128,1,8,4]{2,3,1,0:T(4,128)} %bitcast.5), calls=%async_computation.1 | async-start | bytes 524288 | tf_op jit(solution)/shard_map/all_to_all | solution.py:35
  30.2 227.9 %all-reduce.2.cloned.1.call-start = ((), (), s32[]{:S(2)}) async-start(), calls=%async_computation.4 | async-start | bytes 8388608 | tf_op jit(solution)/shard_map/psum | solution.py:162
  85.6 68.7 %copy-start.1 = (s32[1,256]{1,0:T(1,128)S(1)}, s32[1,256]{1,0:T(1,128)}, u32[]{:S(2)}) copy-start(s32[1,256]{1,0:T(1,128)} %param.13) | copy-start | bytes 3076
  85.6 172.5 %copy-start = (f32[1,2048]{1,0:T(1,128)S(1)}, f32[1,2048]{1,0:T(1,128)}, u32[]{:S(2)}) copy-start(f32[1,2048]{1,0:T(1,128)} %dec.1) | copy-start | bytes 24580
  277.0 11.8 %all-to-all-start.2 = ((bf16[8,2,8192]{2,1,0:T(2,128)(2,1)}), bf16[8,2,8192]{2,1,0:T(2,128)(2,1)S(1)}, u32[]{:S(2)}, u32[]{:S(2)}) async-start(bf16[8,2,8192]{2,1,0:T(2,128)(2,1)} %reshape.317), calls=%async_computation.2 | async-start | bytes 524288 | tf_op jit(solution)/shard_map/all_to_all | solution.py:178
Sparse Core Ops, SparseCore 0:
  19.6 53.9 all-gather.1
  154.5 103.5 all-reduce.1

commit v2 on v0

v2 whole, which is shorter than its diff:
```python
import jax
import jax.numpy as jnp
from jax import lax
from jax.experimental import pallas as pl
from jax.experimental.pallas import tpu as pltpu
from jax.sharding import Mesh
from jax.sharding import PartitionSpec as P

Y, C, X, Z = "layer_0", "layer_1", "lat_0", "lat_1"
LAT = (X, Z)
LAYER = (Y, C)
LAYER_LAT = (Y, C, X, Z)
MESH = pl.DeviceIdType.MESH
NT = (((1,), (1,)), ((), ()))
F32 = jnp.float32
BF16 = jnp.bfloat16
TILE = 1024
STAT = 512
COLS = 1024
TOK = 8
HALF = 32
BLOCK = 256
RES = 8

TO_LAYER, FIRST, NEAR, RELAY, SQUARE, SHARE, SEEDS, LAST, LAST_SEEDS, FINAL, BACK, COUNT = (
    0, 8, 14, 18, 22, 38, 44, 50, 56, 62, 78, 86
)


def row_stats(w, dec, shift, inv, norm, j):
    sq = dc = None
    for g in range(w.shape[1] // 128):
        at = slice(g * 128, (g + 1) * 128)
        piece = w[pl.ds(j * STAT, STAT), at].astype(F32)
        a, b = piece * piece, piece * dec[0:1, at]
        sq, dc = (a, b) if sq is None else (sq + a, dc + b)
    ones = jnp.ones((8, 128), F32)
    hi = lax.Precision.HIGHEST
    total = lax.dot_general(ones, sq, NT, precision=hi, preferred_element_type=F32)
    n = jnp.sqrt(total + 1e-06)
    norm[j] = n
    inv[j] = 1.0 / n
    shift[j] = lax.dot_general(ones, dc, NT, precision=hi, preferred_element_type=F32)


def encode_tile(feats, w, slot, shift, inv, enc, mass, coef, p, j):
    p[...] = lax.dot_general(
        feats[...], w[pl.ds(j * TILE, TILE), :], NT, preferred_element_type=F32
    )
    for g in range(TILE // 128):
        s = j * (TILE // STAT) + g // (STAT // 128)
        at = slice(g % (STAT // 128) * 128, (g % (STAT // 128) + 1) * 128)
        iv = inv[s, :, at]
        pre = p[:, g * 128 : (g + 1) * 128].reshape(BLOCK // 8, 8, 128)
        act = jnp.maximum((pre - shift[s, :, at]) * iv + enc[s, :, at], 0.0)
        base = (j * TILE + g * 128).astype(F32)
        total = None
        for c in range(4):
            hit = jnp.where(slot[c] == base, act, 0.0)
            total = hit if total is None else total + hit
        mass[s, :, at] += jnp.sum(total, axis=0)
        to = pl.ds(pl.multiple_of(j * TILE + g * 128, 128), 128)
        coef[:, to] = (total * iv).reshape(BLOCK, 128).astype(BF16)


def kernel(
    aug, w_hbm, dec, enc, pos, recon, unexplained, mass, new_rows,
    w, own, fa, fb, nf, slot, coef, p, part, ra, rb, seeds, rsa, rsb,
    sa, sb, ta, tb, ssa, ssb, tsa, tsb, squares, finals, shift, inv, norm, rec,
    send, recv, wsem, osem,
):
    d = w.shape[1]
    lats = w.shape[0]
    y, c, x, z = (lax.axis_index(a) for a in (Y, C, X, Z))
    me = 2 * y + c
    tokens = 4 * BLOCK

    def ring(at, step):
        return lax.rem(at + step, 4)

    def push(src, dst, n, device):
        copy = pltpu.make_async_remote_copy(
            src_ref=src, dst_ref=dst, send_sem=send.at[n], recv_sem=recv.at[n],
            device_id=device, device_id_type=MESH,
        )
        return copy

    def local(src, dst, n):
        return pltpu.make_async_copy(src, dst, osem.at[n])

    sent = []

    def start(copies):
        for copy in copies:
            copy.start()
        sent.extend(copies)

    def arrive(copies):
        for copy in copies:
            copy.wait_recv()

    rows = lats // 4
    loads = [
        pltpu.make_async_copy(w_hbm.at[pl.ds(q * rows, rows)], w.at[pl.ds(q * rows, rows)], wsem.at[q])
        for q in range(4)
    ]
    for load in loads:
        load.start()

    column = [(dy, dc) for dy in range(4) for dc in range(2) if dy or dc]
    plane = [(dx, dz) for dx in range(4) for dz in range(4) if dx or dz]

    def in_column(dy, dc):
        return {Y: ring(y, dy), C: lax.rem(c + dc, 2)}

    def in_plane(dx, dz):
        return {X: ring(x, dx), Z: ring(z, dz)}

    barrier = pltpu.get_barrier_semaphore()
    for dy, dc in column:
        pl.semaphore_signal(barrier, inc=1, device_id=in_column(dy, dc), device_id_type=MESH)
    for dx, dz in plane:
        pl.semaphore_signal(barrier, inc=1, device_id=in_plane(dx, dz), device_id_type=MESH)
    pl.semaphore_wait(barrier, len(column) + len(plane))

    to_layer = []
    for dy, dc in column:
        g = 2 * ring(y, dy) + lax.rem(c + dc, 2)
        to_layer.append(push(aug.at[g], own.at[me], TO_LAYER + 2 * dy + dc, in_column(dy, dc)))
    start(to_layer)
    mine = local(aug.at[me], own.at[me], 0)
    mine.start()

    def stats(q):
        loads[q].wait()
        per = rows // STAT
        lax.fori_loop(
            q * per, (q + 1) * per, lambda j, _: row_stats(w, dec, shift, inv, norm, j), None
        )

    stats(0)
    mass[...] = jnp.zeros_like(mass)
    mine.wait()
    arrive(to_layer)

    half = TOK // 2
    first = []
    for k in (1, 3, 2):
        first.append(push(own.at[pl.ds(0, half)], fa.at[z, x], FIRST + k - 1, {X: ring(x, k)}))
        first.append(push(own.at[pl.ds(half, half)], fb.at[x, z], FIRST + 2 + k, {Z: ring(z, k)}))
    start(first)
    keep = [local(own.at[pl.ds(0, half)], fa.at[z, x], 1), local(own.at[pl.ds(half, half)], fb.at[x, z], 2)]
    for copy in keep:
        copy.start()

    def add_squares(g, acc):
        v = own[g, :, pl.ds(0, d)].astype(F32)
        return acc + v * v

    square = jnp.sum(lax.fori_loop(0, TOK, add_squares, jnp.zeros((TOK, d), F32)))
    here = 4 * x + z
    squares[here] = jnp.full((8, 128), square, F32)
    square_copies = [
        push(squares.at[here], squares.at[here], SQUARE + 4 * dx + dz, in_plane(dx, dz))
        for dx, dz in plane
    ]
    start(square_copies)
    stats(1)
    for copy in keep:
        copy.wait()
    arrive(first)
    near = []
    for e, k in enumerate((1, 3)):
        near.append(push(fa.at[z], fa.at[z], NEAR + 2 * e, {Z: ring(z, k)}))
        near.append(push(fb.at[x], fb.at[x], NEAR + 2 * e + 1, {X: ring(x, k)}))
    start(near)
    stats(2)
    stats(3)
    arrive(square_copies)
    scale = lax.rsqrt(jnp.sum(squares[...], axis=0)[0:1, 0:1] / (tokens * d))

    pick_row = lax.broadcasted_iota(jnp.int32, (128, 512), 0)
    pick_slot = lax.broadcasted_iota(jnp.int32, (128, 512), 1) // 128 + 4 * here
    pick = jnp.where(pick_row == pick_slot, 64.0, 0.0) + jnp.where(pick_row == pick_slot + 64, 1.0, 0.0)
    pick = pick.astype(BF16)

    up, down = pl.ds(0, 2), pl.ds(2, 2)
    relay = [
        push(fa.at[ring(z, 3), up], fa.at[ring(z, 3), up], RELAY, {Z: ring(z, 1)}),
        push(fa.at[ring(z, 1), down], fa.at[ring(z, 1), down], RELAY + 1, {Z: ring(z, 3)}),
        push(fb.at[ring(x, 3), up], fb.at[ring(x, 3), up], RELAY + 2, {X: ring(x, 1)}),
        push(fb.at[ring(x, 1), down], fb.at[ring(x, 1), down], RELAY + 3, {X: ring(x, 3)}),
    ]
    sent.extend(relay)

    def share(k):
        return [
            push(part.at[k, pl.ds(0, 128)], ra.at[k - 1], SHARE + k - 1, {Z: ring(z, k)}),
            push(part.at[k, pl.ds(128, 128)], rb.at[k - 1], SHARE + 2 + k, {X: ring(x, k)}),
        ]

    def block(step, _):
        k = step + step // 2 - 2 * (step // 3)

        @pl.when(step == 1)
        def _():
            arrive(near)
            for copy in relay:
                copy.start()

        @pl.when(step == 3)
        def _():
            arrive(relay)

        lane = lax.broadcasted_iota(jnp.int32, (16, 8, 128), 2).astype(F32)
        for h, buf, at in ((0, fa, ring(z, k)), (1, fb, ring(x, k))):

            def normalize(q, _, h=h, buf=buf, at=at):
                v = buf[at, q, :, :, pl.ds(0, d)].astype(F32).reshape(HALF, d) * scale
                nf[k, pl.ds(h * 128 + q * HALF, HALF), :] = v.astype(BF16)

            lax.fori_loop(0, 4, normalize, None)
            tail = buf[at, :, :, :, pl.ds(d, 128)].astype(F32).reshape(128, 128).astype(BF16)
            ids = jnp.dot(tail, pick, preferred_element_type=F32)
            for s in range(4):
                slot[s, pl.ds(16 * h, 16)] = ids[:, s * 128 : (s + 1) * 128].reshape(16, 8, 128) - lane

        lax.fori_loop(
            0,
            lats // TILE,
            lambda j, _: encode_tile(nf.at[k], w, slot, shift, inv, enc, mass, coef, p, j),
            None,
        )

        @pl.loop(0, d // COLS)
        def _(n):
            at = pl.ds(pl.multiple_of(n * COLS, COLS), COLS)
            part[k, :, at] = jnp.dot(coef[...], w[:, at], preferred_element_type=F32).astype(BF16)

        @pl.when(step > 0)
        def _():
            for copy in share(k):
                copy.start()

    lax.fori_loop(0, 4, block, None)
    shares = share(1) + share(3) + share(2)
    sent.extend(shares)

    spots = lax.broadcasted_iota(jnp.int32, (4 * 2 * 4 * RES, 128), 1)
    onehot = jnp.concatenate(
        [jnp.where(pos[...] - q * 128 == spots, 1.0, 0.0) for q in range(tokens // 128)], axis=1
    ).astype(BF16)

    @pl.loop(0, d // 512)
    def _(n):
        at = pl.ds(pl.multiple_of(n * 512, 512), 512)
        v = jnp.dot(onehot, part[:, :, at].reshape(tokens, 512), preferred_element_type=F32)
        seeds[:, :, :, :, at] = v.reshape(4, 2, 4, RES, 512).astype(BF16)

    seed_copies = []
    for k in (2, 1, 3):
        seed_copies.append(push(seeds.at[k, 0], rsa.at[k - 1], SEEDS + k - 1, {Z: ring(z, k)}))
        seed_copies.append(push(seeds.at[k, 1], rsb.at[k - 1], SEEDS + 2 + k, {X: ring(x, k)}))
    start(seed_copies)
    arrive(shares)

    def add_shares(q, _):
        at = pl.ds(q * HALF, HALF)
        for to, got, lo in ((sa, ra, 0), (sb, rb, 128)):
            v = part[0, pl.ds(lo + q * HALF, HALF), :].astype(F32)
            for k in range(3):
                v = v + got[k, at, :].astype(F32)
            to[q] = v.astype(BF16)

    lax.fori_loop(0, 4, add_shares, None)
    last = []
    for k in (1, 3, 2):
        last.append(push(sa.at[ring(x, k)], ta.at[k - 1], LAST + k - 1, {X: ring(x, k)}))
        last.append(push(sb.at[ring(z, k)], tb.at[k - 1], LAST + 2 + k, {Z: ring(z, k)}))
    start(last)
    arrive(seed_copies)

    def add_seeds(q, _):
        for to, got, h in ((ssa, rsa, 0), (ssb, rsb, 1)):
            v = seeds[0, h, q].astype(F32)
            for k in range(3):
                v = v + got[k, q].astype(F32)
            to[q] = v.astype(BF16)

    lax.fori_loop(0, 4, add_seeds, None)
    last_seeds = []
    for k in (1, 3, 2):
        last_seeds.append(push(ssa.at[ring(x, k)], tsa.at[k - 1], LAST_SEEDS + k - 1, {X: ring(x, k)}))
        last_seeds.append(push(ssb.at[ring(z, k)], tsb.at[k - 1], LAST_SEEDS + 2 + k, {Z: ring(z, k)}))
    start(last_seeds)

    def add_tokens(q, acc):
        for k in range(4):
            acc = acc + nf[k, pl.ds(q * 16, 16), :].astype(F32)
        return acc

    sums = lax.fori_loop(0, BLOCK // 16, add_tokens, jnp.zeros((16, d), F32))
    means = jnp.sum(sums, axis=0, keepdims=True) / tokens
    my_pos = jnp.concatenate([pos[pl.ds(x * RES, RES), :], pos[pl.ds(4 * RES + z * RES, RES), :]], axis=0)
    my_spots = lax.broadcasted_iota(jnp.int32, (2 * RES, 128), 1)
    my_onehot = jnp.concatenate(
        [jnp.where(my_pos - q * 128 == my_spots, 1.0, 0.0) for q in range(tokens // 128)], axis=1
    ).astype(BF16)
    seed_feats = jnp.dot(my_onehot, nf[...].reshape(tokens, d), preferred_element_type=F32)
    norm_sum = jnp.sum(norm[...]) / 8.0

    arrive(last)
    numerator = denominator = None
    for h, mine_sum, got, lo in ((0, sa.at[x], ta, x * HALF), (1, sb.at[z], tb, 128 + z * HALF)):
        v = mine_sum[...].astype(F32)
        for k in range(3):
            v = v + got[k].astype(F32)
        v = v + dec[...]
        rec[pl.ds(h * half, half)] = v.reshape(half, TOK, d).astype(BF16)
        feats = nf[0, pl.ds(lo, HALF), :].astype(F32)
        e, m = feats - v, feats - means
        n_h, d_h = jnp.sum(e * e), jnp.sum(m * m)
        numerator = n_h if h == 0 else numerator + n_h
        denominator = d_h if h == 0 else denominator + d_h

    back = []
    for dy, dc in column:
        g = 2 * ring(y, dy) + lax.rem(c + dc, 2)
        back.append(push(rec.at[g], recon.at[me], BACK + 2 * dy + dc, in_column(dy, dc)))
    start(back)
    mine_back = local(rec.at[me], recon.at[me], 0)
    mine_back.start()
    which = lax.broadcasted_iota(jnp.int32, (8, 128), 0)
    finals[here] = jnp.where(which == 0, numerator, jnp.where(which == 1, denominator, norm_sum))
    final_copies = [
        push(finals.at[here], finals.at[here], FINAL + 4 * dx + dz, in_plane(dx, dz)) for dx, dz in plane
    ]
    start(final_copies)

    arrive(last_seeds)
    estimates = []
    for mine_sum, got in ((ssa.at[x], tsa), (ssb.at[z], tsb)):
        v = mine_sum[...].astype(F32)
        for k in range(3):
            v = v + got[k].astype(F32)
        estimates.append(v + dec[...])
    errors = seed_feats - jnp.concatenate(estimates, axis=0)
    seed_norm = jnp.sqrt(jnp.sum(errors * errors, axis=1, keepdims=True) + 1e-06)
    unit = errors / seed_norm
    arrive(final_copies)
    total = jnp.sum(finals[...], axis=0)
    unexplained[...] = jnp.broadcast_to(total[0:1, :] / total[1:2, :], (8, 128))
    new_rows[...] = (unit * (total[2:3, 0:1] / (lats * 16))).astype(BF16)
    mine_back.wait()
    arrive(back)
    for copy in sent:
        copy.wait_send()


def fused(aug, rows, dec, enc, pos):
    lats, d = rows.shape
    wide = aug.shape[2]
    stat = (lats // STAT, 8, STAT)
    enc8 = jnp.broadcast_to(enc.reshape(lats // STAT, 1, STAT), stat)
    vmem = pl.BlockSpec(memory_space=pltpu.VMEM)
    hbm = pl.BlockSpec(memory_space=pl.ANY)
    half = TOK // 2
    scratch = [
        ((lats, d), BF16),
        ((TOK, TOK, wide), BF16),
        ((4, 4, half, TOK, wide), BF16),
        ((4, 4, half, TOK, wide), BF16),
        ((4, BLOCK, d), BF16),
        ((4, BLOCK // 8, 8, 128), F32),
        ((BLOCK, lats), BF16),
        ((BLOCK, TILE), F32),
        ((4, BLOCK, d), BF16),
        ((3, 128, d), BF16),
        ((3, 128, d), BF16),
        ((4, 2, 4, RES, d), BF16),
        ((3, 4, RES, d), BF16),
        ((3, 4, RES, d), BF16),
        ((4, HALF, d), BF16),
        ((4, HALF, d), BF16),
        ((3, HALF, d), BF16),
        ((3, HALF, d), BF16),
        ((4, RES, d), BF16),
        ((4, RES, d), BF16),
        ((3, RES, d), BF16),
        ((3, RES, d), BF16),
        ((16, 8, 128), F32),
        ((16, 8, 128), F32),
        (stat, F32),
        (stat, F32),
        (stat, F32),
        ((TOK, TOK, d), BF16),
    ]
    return pl.pallas_call(
        kernel,
        out_shape=(
            jax.ShapeDtypeStruct((TOK, TOK, d), BF16),
            jax.ShapeDtypeStruct((8, 128), F32),
            jax.ShapeDtypeStruct(stat, F32),
            jax.ShapeDtypeStruct((2 * RES, d), BF16),
        ),
        in_specs=[hbm, hbm, vmem, vmem, vmem],
        out_specs=(vmem, vmem, vmem, vmem),
        scratch_shapes=[pltpu.VMEM(*s) for s in scratch]
        + [
            pltpu.SemaphoreType.DMA((COUNT,)),
            pltpu.SemaphoreType.DMA((COUNT,)),
            pltpu.SemaphoreType.DMA((4,)),
            pltpu.SemaphoreType.DMA((3,)),
        ],
        compiler_params=pltpu.CompilerParams(
            collective_id=0, has_side_effects=True, vmem_limit_bytes=60 * 2**20
        ),
        name="sae",
    )(aug, rows, dec, enc8, pos)


def seed_positions(seed_tokens, x, z):
    s = seed_tokens.reshape(4, 4, 2, RES)
    roll = lambda v, by: lax.dynamic_slice_in_dim(jnp.concatenate([v, v], 0), by, 4, 0)
    along_z = roll(s[:, :, 0].transpose(1, 0, 2), z)
    along_x = roll(s[:, :, 1], x)
    n = jnp.stack([along_z, along_x], 1).reshape(-1)
    home = n // TOK % 16
    xi, zi, g, t = home // 4, home % 4, n // (16 * TOK), n % TOK
    a = (zi - z) % 4 * BLOCK + xi * HALF + g * TOK + t
    b = (xi - x) % 4 * BLOCK + 128 + zi * HALF + (g - TOK // 2) * TOK + t
    pos = jnp.where(g < TOK // 2, a, b)
    return jnp.broadcast_to(pos[:, None], (pos.shape[0], 128))


def body(residuals, topk_slots, dictionary, enc_bias, dec_bias, dead_ids, seed_tokens):
    lat_dev = dictionary.shape[1]
    x, z = lax.axis_index(X), lax.axis_index(Z)
    shard = jnp.arange(topk_slots.shape[2], dtype=jnp.int32) // 4
    place = jnp.where(topk_slots >= 0, topk_slots - shard * lat_dev, lat_dev)
    aug = jnp.concatenate(
        [residuals, (place // 64).astype(BF16), (place % 64).astype(BF16)], axis=2
    )
    pos = seed_positions(seed_tokens[0], x, z)
    recon, unexplained, mass, new_rows = fused(aug, dictionary[0], dec_bias, enc_bias[0], pos)
    latent_mass = jnp.sum(mass, axis=1).reshape(1, lat_dev)
    candidates = (4 * x + z) * lat_dev + jnp.arange(lat_dev, dtype=jnp.int32)
    is_dead = jnp.any(dead_ids[0][:, None] == candidates[None, :], axis=0)
    new_bias = jnp.where(is_dead, 0.0, enc_bias[0])[None]
    return (recon, unexplained[0, 0:1], latent_mass, new_rows[None], new_bias)


def solution(mesh):
    split = Mesh(mesh.devices.reshape(4, 2, 4, 4), (Y, C, X, Z))
    placed = (
        P(None, LAYER_LAT, None),
        P(None, LAYER_LAT, None),
        P(LAYER, LAT, None),
        P(LAYER, LAT),
        P(LAYER, None),
        P(LAYER, None),
        P(LAYER, None),
    )
    return jax.shard_map(
        body,
        mesh=split,
        in_specs=placed,
        out_specs=(
            P(None, LAYER_LAT, None),
            P(LAYER),
            P(LAYER, LAT),
            P(LAYER, LAT, None),
            P(LAYER, LAT),
        ),
        check_vma=False,
    )
```

time: 443 us -> 130 us (0.29)
  local copies, waits for them, and re-layouts: 123 us -> 9.35 us
  Pallas kernels: 0 us -> 113 us
  matrix products: 102 us -> 0 us
  waiting for transfers between devices: 76.3 us -> 0 us
  other arithmetic: 63.9 us -> 6.47 us
  blocking collectives: 46.1 us -> 0 us
  between operations: 17.7 us -> 0.72 us
  starting transfers between devices: 9.27 us -> 0 us
    pallas_call x0 -> x1, Pallas kernels: none -> 113 us  [fused(): pl.pallas_call(kernel, out_shape=(jax.ShapeDtypeStruct((TOK, TOK, d), BF1...]
    gather x8 -> x0, local copies, waits for them, and re-layouts: 112 us -> none  [the longest x4 46.1 us: body(): preact = (products - shifts[clipped]) / picked_norms + enc_bias[0][clipped]]
    dot_general x3 -> x0, matrix products: 102 us -> none  [the longest x1 46 us: body(): jnp.einsum('td,ctd->ct', features, picked, preferred_element_type=jnp.flo...]
    psum x1 -> x0, waiting for transfers between devices: 76.2 us -> none  [body(): lax.psum(partial_value.astype(jnp.bfloat16), LAT).astype(jnp.float32)]
    psum x4 -> x0, blocking collectives: 35.5 us -> none  [one_axis_at_a_time(): return functools.reduce(lax.psum, axes, shard)]
    scatter-add x1 -> x0, other arithmetic: 22.9 us -> none  [body(): jnp.zeros((lat_dev,), jnp.float32).at[clipped.reshape(-1)]]
    reduce_sum x6 -> x1, other arithmetic: 18.4 us -> 0.94 us  [body(): latent_mass = jnp.sum(mass, axis=1).reshape(1, lat_dev)]
    select_n x4 -> x1, other arithmetic: 14.9 us -> 0.04 us  [seed_positions(): pos = jnp.where(g < TOK // 2, a, b)]
  transfers between devices with their start and end apart: 4 -> 0, of which waited for: 1 -> 0; matrix products, arithmetic and copies ran while one was open for 41% -> 0% of each run, Pallas kernels for 0% -> 0%
where the time goes in v2:
time: 130 us; the launch traced here: 129 us
  Pallas kernels  113 us (87%)
  local copies, waits for them, and re-layouts  9.35 us (7%)
  other arithmetic  6.47 us (5%)
    pallas_call x1, Pallas kernels, fused(): pl.pallas_call(kernel, out_shape=(jax.ShapeDtypeStruct((TOK, TOK, d), BF1...  113 us
    unnamed x5, local copies, waits for them, and re-layouts  4.79 us

profile of v2, /device:TPU:0, one launch (start us, length us, event | category | flops | bytes accessed | tf_op | source)
XLA Modules:
  0.0 129.1 jit_solution(17969180259185347181)
XLA Ops:
  0.6 0.5 broadcast.318
  1.2 1.3 %reduce.7 = s32[256]{0:T(256)S(1)} reduce(s32[1,256]{1,0:T(1,128)} %param.13, s32[]{:T(128)} %broadcast.318), dimensions={0}, to_apply=%param.13.reduce_sub_computation.3 | reduce | bytes 2052 | tf_op args[6]
  2.5 0.1 reshape_squeeze.4
  2.7 0.1 reshape.172
  2.9 1.3 compare_reduce_fusion
  4.2 0.5 broadcast.317
  4.7 2.0 %reshape_select_fusion = (f32[1,4096]{1,0:T(1,128)}, f32[4096]{0:T(1024)S(1)}) fusion(f32[1,4096]{1,0:T(1,128)} %param.10, pred[4096]{0:T(1024)(128)(4,1)S(1)} %compare_reduce_fusion, f32[]{:T(128)} %broadcast.317), kind=kLoop, calls=%fused_computation.1 | loop fusion | flops 4096 | bytes 53252 | tf_op jit(solution)/shard_map/jit(_where)/select_n | solution.py:449
  6.7 0.8 fusion.1
  7.5 0.7 broadcast_in_dim.29.enc
  8.1 0.8 broadcast_in_dim.30.pos
  8.9 1.7 %concatenate.9.aug = bf16[8,8,2176]{2,1,0:T(8,128)(2,1)} concatenate(bf16[8,8,2048]{2,1,0:T(8,128)(2,1)} %param.7, bf16[8,8,64]{2,1,0:T(8,128)(2,1)S(1)} %get-tuple-element.14, bf16[8,8,64]{2,1,0:T(8,128)(2,1)S(1)} %get-tuple-element.13), dimensions={2} | concatenate | bytes 557056 | tf_op jit(solution)/shard_map/concatenate | solution.py:441
  10.6 112.6 %sae.1 = (bf16[8,8,2048]{2,1,0:T(8,128)(2,1)}, f32[8,128]{1,0:T(8,128)}, f32[8,8,512]{2,1,0:T(8,128)}, bf16[16,2048]{1,0:T(8,128)(2,1)}) custom-call(bf16[8,8,2176]{2,1,0:T(8,128)(2,1)} %concatenate.9.aug, bf16[4096,2048]{1,0:T(8,128)(2,1)} %bitcast.19, f32[1,2048]{1,0:T(1,128)} %dec.1, f32[8,8,512]{2,1,0:T(8,128)} %broadcast_in_dim.29.enc, ...), custom_call_target="tpu_custom_call" | custom-call | tf_op jit(solution)/shard_map/sae/pallas_call | solution.py:398
  123.2 1.2 slice.11
  124.4 0.9 reduce_sum.9
  125.4 0.6 copy.25
  126.0 1.7 %copy.29 = bf16[8,8,2048]{2,1,0:T(8,128)(2,1)} copy(bf16[8,8,2048]{2,1,0:T(8,128)(2,1)} %get-tuple-element.26) | data formatting | bytes 524288
  127.7 1.5 %copy.30 = bf16[1,16,2048]{2,1,0:T(8,128)(2,1)} copy(bf16[1,16,2048]{2,1,0:T(8,128)(2,1)} %bitcast.21) | data formatting | bytes 131072
  (9 shorter events, 0.1 us)

commit v3 on v2

v3 whole, which is shorter than its diff:
```python
import jax
import jax.numpy as jnp
from jax import lax
from jax.experimental import pallas as pl
from jax.experimental.pallas import tpu as pltpu
from jax.sharding import Mesh
from jax.sharding import PartitionSpec as P

Y, C, X, Z = "layer_0", "layer_1", "lat_0", "lat_1"
LAT = (X, Z)
LAYER = (Y, C)
LAYER_LAT = (Y, C, X, Z)
MESH = pl.DeviceIdType.MESH
NT = (((1,), (1,)), ((), ()))
F32 = jnp.float32
BF16 = jnp.bfloat16
TILE = 1024
STAT = 512
COLS = 1024
TOK = 8
HALF = 32
BLOCK = 256
RES = 8
GROUPS = TILE // 128

TO_LAYER, FIRST, AROUND, SQUARE, FAR, NEAR, SEEDS, LAST, LAST_SEEDS, FINAL, BACK, COUNT = (
    0, 8, 14, 24, 40, 42, 50, 56, 68, 74, 90, 98
)


def row_stats(w, decs, enc, inv, bias, norm, j):
    sq = None
    tile = pl.ds(j * STAT, STAT)
    for g in range(w.shape[1] // 128):
        piece = w[tile, g * 128 : (g + 1) * 128].astype(F32)
        a = piece * piece
        sq = a if sq is None else sq + a
    ones = jnp.ones((8, 128), F32)
    total = lax.dot_general(
        ones, sq, NT, precision=lax.Precision.HIGHEST, preferred_element_type=F32
    )
    parts = lax.dot_general(decs[...], w[tile, :], NT, preferred_element_type=F32)
    shift = jnp.sum(parts, axis=0, keepdims=True)
    n = jnp.sqrt(total + 1e-06)
    norm[...] += n
    iv = 1.0 / n
    for g in range(STAT // 128):
        at = slice(g * 128, (g + 1) * 128)
        row = j * (STAT // 128) + g
        inv[row] = iv[:, at]
        bias[row] = enc[pl.ds(row, 1), :] - shift[:, at] * iv[:, at]


def encode(feats, w, bits, inv, bias, mass, coef, p, between):
    tiles = w.shape[0] // TILE

    def product(j):
        p[j % 2] = lax.dot_general(
            feats[...], w[pl.ds(j * TILE, TILE), :], NT, preferred_element_type=F32
        )

    def activity(j):
        for g in range(GROUPS):
            row = j * GROUPS + g
            iv = inv[row]
            pre = p[j % 2, :, g * 128 : (g + 1) * 128].reshape(BLOCK // 8, 8, 128)
            count = ((bits[j] >> (4 * g)) & 15).astype(F32)
            total = jnp.maximum(pre * iv + bias[row], 0.0) * count
            mass[row] += jnp.sum(total, axis=0)
            coef[:, row * 128 : (row + 1) * 128] = (total * iv).reshape(BLOCK, 128).astype(BF16)

    product(0)
    for j in range(1, tiles):
        product(j)
        activity(j - 1)
        if j == 1:
            between()
    activity(tiles - 1)


def iota(shape, dim):
    return lax.broadcasted_iota(jnp.int32, shape, dim)


def seed_places(seeds, x, z):
    n = seeds[...]
    home, g, t = (n >> 3) & 15, n >> 7, n & 7
    xi, zi = home >> 2, home & 3
    is_a = g < 4
    far = jnp.where(is_a, zi - z, xi - x) & 3
    index = jnp.where(is_a, xi, zi)
    odd = (far & 1) == 1
    step = jnp.where(odd, 1 + ((g & 3) >> 1 << 1), far)
    inside = jnp.where(
        odd, (far >> 1) * 64 + index * 16 + (g & 1) * TOK, index * HALF + (g & 3) * TOK
    )
    place = step * BLOCK + jnp.where(is_a, 0, 128) + inside + t
    size = seeds.shape[1]
    row, col = iota((size, size), 0), iota((size, size), 1)
    k, h, i = row >> 6, (row >> 5) & 1, (row >> 3) & 3
    xr = jnp.where(h == 0, i, (x + k) & 3)
    zr = jnp.where(h == 0, (z + k) & 3, i)
    match = col == (xr * 4 + zr) * 16 + h * RES + (row & 7)
    ones = jnp.ones((size, 128), BF16)

    def column(v):
        kept = jnp.where(match, v.astype(F32), 0.0).astype(BF16)
        return jnp.dot(kept, ones, preferred_element_type=F32)

    return column(place >> 5) * 32.0 + column(place & 31)


def one_hot(places, count):
    spots = iota(places.shape, 1).astype(F32)
    return jnp.concatenate(
        [jnp.where(places - q * 128.0 == spots, 1.0, 0.0) for q in range(count // 128)], axis=1
    ).astype(BF16)


def kernel(
    res, slots, w_hbm, dec, enc, dead, seed_tokens,
    recon, unexplained, mass_out, new_rows, new_bias,
    w, aug, own, fa, fb, nf, bits, coef, p, part, fara, farb, near_in, picked, seeds, rsa, rsb,
    sa, sb, ta, tb, ssa, ssb, tsa, tsb, squares, finals, inv, bias, norm, mass, decs, places, rec,
    send, recv, wsem, osem,
):
    d = w.shape[1]
    lats = w.shape[0]
    y, c, x, z = (lax.axis_index(a) for a in (Y, C, X, Z))
    me = 2 * y + c
    here = 4 * x + z
    tokens = 4 * BLOCK

    def ring(at, step):
        return lax.rem(at + step, 4)

    def push(src, dst, n, device):
        return pltpu.make_async_remote_copy(
            src_ref=src, dst_ref=dst, send_sem=send.at[n], recv_sem=recv.at[n],
            device_id=device, device_id_type=MESH,
        )

    def local(src, dst, n):
        return pltpu.make_async_copy(src, dst, osem.at[n])

    sent = []

    def start(copies):
        for copy in copies:
            copy.start()
        sent.extend(copies)

    def arrive(copies):
        for copy in copies:
            copy.wait_recv()

    column = [(dy, dc) for dy in range(4) for dc in range(2) if dy or dc]
    plane = [(dx, dz) for dx in range(4) for dz in range(4) if dx or dz]

    def in_column(dy, dc):
        return {Y: ring(y, dy), C: lax.rem(c + dc, 2)}

    def in_plane(dx, dz):
        return {X: ring(x, dx), Z: ring(z, dz)}

    barrier = pltpu.get_barrier_semaphore()
    for dy, dc in column:
        pl.semaphore_signal(barrier, inc=1, device_id=in_column(dy, dc), device_id_type=MESH)
    for dx, dz in plane:
        pl.semaphore_signal(barrier, inc=1, device_id=in_plane(dx, dz), device_id_type=MESH)

    fill = local(res, aug.at[:, :, pl.ds(0, d)], 0)
    fill.start()
    rows = lats // 4
    loads = [
        pltpu.make_async_copy(w_hbm.at[pl.ds(q * rows, rows)], w.at[pl.ds(q * rows, rows)], wsem.at[q])
        for q in range(4)
    ]
    ids = slots[...]
    place = jnp.where(ids >= 0, ids - (iota(ids.shape, 2) >> 2) * lats, lats)
    tail = jnp.concatenate([(place >> 6).astype(F32), (place & 63).astype(F32)], axis=2)
    aug[:, :, pl.ds(d, 128)] = tail.astype(BF16)
    fill.wait()
    pl.semaphore_wait(barrier, len(column) + len(plane))

    to_layer = []
    for dy, dc in column:
        g = 2 * ring(y, dy) + lax.rem(c + dc, 2)
        to_layer.append(push(aug.at[g], own.at[me], TO_LAYER + 2 * dy + dc, in_column(dy, dc)))
    start(to_layer)
    for load in loads:
        load.start()
    own[me] = aug[me]

    high = dec[...].astype(BF16).astype(F32)
    middle = (dec[...] - high).astype(BF16).astype(F32)
    low = dec[...] - high - middle
    which = iota((16, d), 0)
    decs[...] = jnp.where(
        which == 0, high, jnp.where(which == 1, middle, jnp.where(which == 2, low, 0.0))
    ).astype(BF16)
    norm[...] = jnp.zeros_like(norm)
    mass[...] = jnp.zeros_like(mass)

    def stats(q):
        loads[q].wait()
        per = rows // STAT
        lax.fori_loop(
            q * per, (q + 1) * per, lambda j, _: row_stats(w, decs, enc, inv, bias, norm, j), None
        )

    stats(0)
    arrive(to_layer)

    half = TOK // 2
    first = []
    for k in (1, 3, 2):
        first.append(push(own.at[pl.ds(0, half)], fa.at[z, x], FIRST + k - 1, {X: ring(x, k)}))
        first.append(push(own.at[pl.ds(half, half)], fb.at[x, z], FIRST + 2 + k, {Z: ring(z, k)}))
    start(first)
    fa[z, x] = own[pl.ds(0, half)]
    fb[x, z] = own[pl.ds(half, half)]

    def add_squares(g, acc):
        v = own[g, :, pl.ds(0, d)].astype(F32)
        return acc + v * v

    square = jnp.sum(lax.fori_loop(0, TOK, add_squares, jnp.zeros((TOK, d), F32)))
    squares[here] = jnp.full((8, 128), square, F32)
    square_copies = [
        push(squares.at[here], squares.at[here], SQUARE + 4 * dx + dz, in_plane(dx, dz))
        for dx, dz in plane
    ]
    start(square_copies)
    stats(1)
    arrive(first)

    def beside(h):
        rows = pl.ds(2 * h, 2)
        out = []
        for e, k in enumerate((1, 3)):
            n = AROUND + 2 + 4 * h + 2 * e
            out.append(push(fa.at[z, :, rows], fa.at[z, :, rows], n, {Z: ring(z, k)}))
            out.append(push(fb.at[x, :, rows], fb.at[x, :, rows], n + 1, {X: ring(x, k)}))
        return out

    across = [
        push(fa.at[z], fa.at[z], AROUND, {Z: ring(z, 2)}),
        push(fb.at[x], fb.at[x], AROUND + 1, {X: ring(x, 2)}),
    ]
    beside_a, beside_b = beside(0), beside(1)
    start(beside_a)
    sent.extend(across + beside_b)
    stats(2)
    stats(3)
    places[...] = seed_places(seed_tokens, x, z)
    arrive(square_copies)
    scale = lax.rsqrt(jnp.sum(squares[...], axis=0)[0:1, 0:1] / (tokens * d))

    pick_row = iota((128, 512), 0)
    pick_slot = (iota((128, 512), 1) >> 7) + 4 * here
    pick = jnp.where(pick_row == pick_slot, 64.0, 0.0) + jnp.where(pick_row == pick_slot + 64, 1.0, 0.0)
    pick = pick.astype(BF16)

    def near_share(h):
        devices = ({Z: ring(z, 1)}, {Z: ring(z, 3)}, {X: ring(x, 1)}, {X: ring(x, 3)})
        return [
            push(part.at[1 + 2 * h, pl.ds(e * 64, 64)], near_in.at[h, e], NEAR + 4 * h + e, device)
            for e, device in enumerate(devices)
        ]

    near_a, near_b = near_share(0), near_share(1)
    far = [
        push(part.at[2, pl.ds(0, 128)], fara, FAR, {Z: ring(z, 2)}),
        push(part.at[2, pl.ds(128, 128)], farb, FAR + 1, {X: ring(x, 2)}),
    ]
    sent.extend(far + near_a + near_b)

    def decode(step, source):
        @pl.loop(0, d // COLS)
        def _(n):
            at = pl.ds(pl.multiple_of(n * COLS, COLS), COLS)
            v = jnp.dot(source[...], w[:, at], preferred_element_type=F32)
            part[step, :, at] = v.astype(BF16)

    def block(step, _):
        close = step % 2

        @pl.when(step == 1)
        def _():
            arrive(beside_a)

        @pl.when(step == 2)
        def _():
            arrive(across)

        @pl.when(step == 3)
        def _():
            arrive(beside_b)

        lane = iota((16, 8, 128), 2)
        for h, buf, at in ((0, fa, z), (1, fb, x)):

            def chunk(m, cols):
                away = (1 - close) * step + close * (1 + m // 4 * 2)
                index = (1 - close) * (m // 2) + close * (m % 4)
                low = (1 - close) * (m % 2 * 2) + close * (step - 1)
                v = buf[ring(at, away), index, pl.ds(low, 2), :, cols]
                return v.astype(F32).reshape(16, cols.size)

            def normalize(m, _, h=h, chunk=chunk):
                v = chunk(m, pl.ds(0, d)) * scale
                nf[step, pl.ds(h * 128 + m * 16, 16), :] = v.astype(BF16)

            lax.fori_loop(0, 8, normalize, None)
            tails = [chunk(m, pl.ds(d, 128)) for m in range(8)]
            tails = jnp.concatenate(tails, axis=0).astype(BF16)
            found = jnp.dot(tails, pick, preferred_element_type=F32).astype(jnp.int32)
            fields = [jnp.zeros((16, 8, 128), jnp.int32) for _ in range(lats // TILE)]
            for s in range(4):
                v = found[:, s * 128 : (s + 1) * 128].reshape(16, 8, 128)
                one = jnp.where((v & 127) == lane, jnp.int32(1) << (((v >> 7) & 7) << 2), 0)
                fields = [f + jnp.where(v >> 10 == j, one, 0) for j, f in enumerate(fields)]
            for j, f in enumerate(fields):
                bits[j, pl.ds(16 * h, 16)] = f

        def between():
            @pl.when(step == 0)
            def _():
                for copy in across:
                    copy.start()

        mine = jnp.minimum(step, 1)
        encode(nf.at[step], w, bits, inv, bias, mass, coef.at[mine], p, between)

        @pl.when(step == 1)
        def _():
            for copy in beside_b:
                copy.start()

        @pl.when(step > 0)
        def _():
            decode(step, coef.at[1])

        @pl.when(step == 1)
        def _():
            for copy in near_a:
                copy.start()

        @pl.when(step == 2)
        def _():
            for copy in far:
                copy.start()

        @pl.when(step == 3)
        def _():
            for copy in near_b:
                copy.start()

    lax.fori_loop(0, 4, block, None)

    hot = one_hot(places[...], tokens)

    @pl.loop(0, d // 512)
    def _(n):
        at = pl.ds(pl.multiple_of(n * 512, 512), 512)
        others = part[1:, :, at].reshape(3 * BLOCK, 512)
        picked[:, at] = jnp.dot(hot[:, BLOCK:], others, preferred_element_type=F32)

    decode(0, coef.at[0])

    def combine(h):
        for i in range(4):
            at, in_h = pl.ds(i * HALF + h * 16, 16), pl.ds(i * 16, 16)
            for to, got, lo, e in ((sa, fara, 0, 0), (sb, farb, 128, 2)):
                v = part[0, pl.ds(lo + i * HALF + h * 16, 16), :].astype(F32) + got[at, :].astype(F32)
                v = v + near_in[h, e, in_h, :].astype(F32) + near_in[h, e + 1, in_h, :].astype(F32)
                to[h, i] = v.astype(BF16)
        copies = []
        for k in (2, 1, 3):
            n = LAST + 6 * h + k - 1
            copies.append(push(sa.at[h, ring(x, k)], ta.at[h, k - 1], n, {X: ring(x, k)}))
            copies.append(push(sb.at[h, ring(z, k)], tb.at[h, k - 1], n + 3, {Z: ring(z, k)}))
        start(copies)
        return copies

    arrive(far)
    arrive(near_a)
    last = [combine(0)]

    @pl.loop(0, d // 512)
    def _(n):
        at = pl.ds(pl.multiple_of(n * 512, 512), 512)
        v = jnp.dot(hot[:, :BLOCK], part[0, :, at], preferred_element_type=F32) + picked[:, at]
        seeds[:, :, :, :, at] = v.reshape(4, 2, 4, RES, 512).astype(BF16)

    seed_copies = []
    for k in (2, 1, 3):
        seed_copies.append(push(seeds.at[k, 0], rsa.at[k - 1], SEEDS + k - 1, {Z: ring(z, k)}))
        seed_copies.append(push(seeds.at[k, 1], rsb.at[k - 1], SEEDS + 2 + k, {X: ring(x, k)}))
    arrive(near_b)
    last.append(combine(1))
    start(seed_copies)

    def add_tokens(q, acc):
        for k in range(4):
            acc = acc + nf[k, pl.ds(q * 16, 16), :].astype(F32)
        return acc

    sums = lax.fori_loop(0, BLOCK // 16, add_tokens, jnp.zeros((16, d), F32))
    means = jnp.sum(sums, axis=0, keepdims=True) / tokens
    my_places = jnp.concatenate(
        [places[pl.ds(x * RES, RES), :], places[pl.ds(4 * RES + z * RES, RES), :]], axis=0
    )
    seed_feats = jnp.dot(
        one_hot(my_places, tokens), nf[...].reshape(tokens, d), preferred_element_type=F32
    )
    norm_sum = jnp.sum(norm[...]) / 8.0

    def back(g):
        device = {Y: g // 2 + 0 * y, C: g % 2 + 0 * c}
        return pltpu.make_async_remote_copy(
            src_ref=rec.at[g], dst_ref=recon.at[me], send_sem=send.at[BACK + g],
            recv_sem=recv.at[BACK + me], device_id=device, device_id_type=MESH,
        )

    def elsewhere(g, act):
        @pl.when(me != g)
        def _():
            act()

    numerator = denominator = 0.0
    for h in range(2):
        arrive(last[h])
        for mine_sum, got, g, lo in (
            (sa.at[h, x], ta, 2 * h, x * HALF),
            (sb.at[h, z], tb, half + 2 * h, 128 + z * HALF),
        ):
            v = mine_sum[...].astype(F32)
            for k in range(3):
                v = v + got[h, k].astype(F32)
            v = v + dec[...]
            rec[pl.ds(g, 2)] = v.reshape(2, TOK, d).astype(BF16)
            for e in (g, g + 1):
                elsewhere(e, lambda e=e: back(e).start())
            feats = nf[0, pl.ds(lo + 16 * h, 16), :].astype(F32)
            e, m = feats - v, feats - means
            numerator = numerator + jnp.sum(e * e)
            denominator = denominator + jnp.sum(m * m)
    recon[me] = rec[me]
    kind = iota((8, 128), 0)
    finals[here] = jnp.where(kind == 0, numerator, jnp.where(kind == 1, denominator, norm_sum))
    final_copies = [
        push(finals.at[here], finals.at[here], FINAL + 4 * dx + dz, in_plane(dx, dz)) for dx, dz in plane
    ]
    start(final_copies)
    arrive(seed_copies)

    def add_seeds(q, _):
        for to, got, h in ((ssa, rsa, 0), (ssb, rsb, 1)):
            v = seeds[0, h, q].astype(F32)
            for k in range(3):
                v = v + got[k, q].astype(F32)
            to[q] = v.astype(BF16)

    lax.fori_loop(0, 4, add_seeds, None)
    last_seeds = []
    for k in (1, 3, 2):
        last_seeds.append(push(ssa.at[ring(x, k)], tsa.at[k - 1], LAST_SEEDS + k - 1, {X: ring(x, k)}))
        last_seeds.append(push(ssb.at[ring(z, k)], tsb.at[k - 1], LAST_SEEDS + 2 + k, {Z: ring(z, k)}))
    start(last_seeds)

    lanes = lats // 128
    gone = dead[...] - here * lats
    at_row = jnp.where(iota((lanes, gone.shape[1]), 0) == gone >> 7, 1.0, 0.0).astype(BF16)
    at_lane = jnp.where(iota((128, gone.shape[1]), 0) == (gone & 127), 1.0, 0.0).astype(BF16)
    hits = lax.dot_general(at_row, at_lane, NT, preferred_element_type=F32)
    new_bias[...] = jnp.where(hits > 0.5, 0.0, enc[...])
    mass_out[...] = jnp.sum(mass[...], axis=1)

    arrive(last_seeds)
    estimates = []
    for mine_sum, got in ((ssa.at[x], tsa), (ssb.at[z], tsb)):
        v = mine_sum[...].astype(F32)
        for k in range(3):
            v = v + got[k].astype(F32)
        estimates.append(v + dec[...])
    errors = seed_feats - jnp.concatenate(estimates, axis=0)
    seed_norm = jnp.sqrt(jnp.sum(errors * errors, axis=1, keepdims=True) + 1e-06)
    unit = errors / seed_norm
    arrive(final_copies)
    total = jnp.sum(finals[...], axis=0)
    ratio = total[0:1, :] / total[1:2, :]
    unexplained[0] = ratio[0, 0]
    new_rows[...] = (unit * (total[2:3, 0:1] / (lats * 16))).astype(BF16)
    for g in range(TOK):
        def settle(g=g):
            pltpu.make_async_remote_copy(
                src_ref=rec.at[g], dst_ref=recon.at[g], send_sem=send.at[BACK + g],
                recv_sem=recv.at[BACK + g], device_id={Y: ring(y, 1)}, device_id_type=MESH,
            ).wait()

        elsewhere(g, settle)
    for copy in sent:
        copy.wait_send()


def hand_over(*refs):
    count = len(refs) // 2
    refs[count][0] = refs[0][0]
    for i in range(1, count):
        refs[count + i][...] = refs[i][...]


def handed_over(*arrays):
    specs = [pl.BlockSpec(memory_space=pltpu.SMEM)]
    specs += [pl.BlockSpec(memory_space=pltpu.VMEM)] * (len(arrays) - 1)
    return pl.pallas_call(
        hand_over,
        out_shape=tuple(jax.ShapeDtypeStruct(a.shape, a.dtype) for a in arrays),
        in_specs=specs,
        out_specs=tuple(specs),
        name="hand_over",
    )(*arrays)


def fused(residuals, slots, rows, dec, enc, dead, seed_tokens):
    lats, d = rows.shape
    wide = d + 128
    lanes = lats // 128
    vmem = pl.BlockSpec(memory_space=pltpu.VMEM)
    hbm = pl.BlockSpec(memory_space=pl.ANY)
    half = TOK // 2
    scratch = [
        ((lats, d), BF16),
        ((TOK, TOK, wide), BF16),
        ((TOK, TOK, wide), BF16),
        ((4, 4, half, TOK, wide), BF16),
        ((4, 4, half, TOK, wide), BF16),
        ((4, BLOCK, d), BF16),
        ((lats // TILE, BLOCK // 8, 8, 128), jnp.int32),
        ((2, BLOCK, lats), BF16),
        ((2, BLOCK, TILE), F32),
        ((4, BLOCK, d), BF16),
        ((128, d), BF16),
        ((128, d), BF16),
        ((2, 4, 64, d), BF16),
        ((seed_tokens.shape[1], d), F32),
        ((4, 2, 4, RES, d), BF16),
        ((3, 4, RES, d), BF16),
        ((3, 4, RES, d), BF16),
        ((2, 4, HALF // 2, d), BF16),
        ((2, 4, HALF // 2, d), BF16),
        ((2, 3, HALF // 2, d), BF16),
        ((2, 3, HALF // 2, d), BF16),
        ((4, RES, d), BF16),
        ((4, RES, d), BF16),
        ((3, RES, d), BF16),
        ((3, RES, d), BF16),
        ((16, 8, 128), F32),
        ((16, 8, 128), F32),
        ((lanes, 8, 128), F32),
        ((lanes, 8, 128), F32),
        ((8, STAT), F32),
        ((lanes, 8, 128), F32),
        ((16, d), BF16),
        ((seed_tokens.shape[1], 128), F32),
        ((TOK, TOK, d), BF16),
    ]
    return pl.pallas_call(
        kernel,
        out_shape=(
            jax.ShapeDtypeStruct((TOK, TOK, d), BF16),
            jax.ShapeDtypeStruct((1,), F32),
            jax.ShapeDtypeStruct((lanes, 128), F32),
            jax.ShapeDtypeStruct((2 * RES, d), BF16),
            jax.ShapeDtypeStruct((lanes, 128), F32),
        ),
        in_specs=[hbm, vmem, hbm, vmem, vmem, vmem, vmem],
        out_specs=(vmem, pl.BlockSpec(memory_space=pltpu.SMEM), vmem, vmem, vmem),
        scratch_shapes=[pltpu.VMEM(*s) for s in scratch]
        + [
            pltpu.SemaphoreType.DMA((COUNT,)),
            pltpu.SemaphoreType.DMA((COUNT,)),
            pltpu.SemaphoreType.DMA((4,)),
            pltpu.SemaphoreType.DMA((1,)),
        ],
        compiler_params=pltpu.CompilerParams(
            collective_id=0, has_side_effects=True, vmem_limit_bytes=60 * 2**20
        ),
        name="sae",
    )(residuals, slots, rows, dec, enc.reshape(lanes, 128), dead, seed_tokens)


def body(residuals, topk_slots, dictionary, enc_bias, dec_bias, dead_ids, seed_tokens):
    recon, unexplained, mass, new_rows, new_bias = fused(
        residuals, topk_slots, dictionary[0], dec_bias, enc_bias, dead_ids, seed_tokens
    )
    unexplained, recon, mass, new_rows, new_bias = handed_over(
        unexplained, recon, mass, new_rows, new_bias
    )
    return (recon, unexplained, mass.reshape(1, -1), new_rows[None], new_bias.reshape(1, -1))


def solution(mesh):
    split = Mesh(mesh.devices.reshape(4, 2, 4, 4), (Y, C, X, Z))
    placed = (
        P(None, LAYER_LAT, None),
        P(None, LAYER_LAT, None),
        P(LAYER, LAT, None),
        P(LAYER, LAT),
        P(LAYER, None),
        P(LAYER, None),
        P(LAYER, None),
    )
    return jax.shard_map(
        body,
        mesh=split,
        in_specs=placed,
        out_specs=(
            P(None, LAYER_LAT, None),
            P(LAYER),
            P(LAYER, LAT),
            P(LAYER, LAT, None),
            P(LAYER, LAT),
        ),
        check_vma=False,
    )
```

time: 130 us -> 99.7 us (0.77)
  Pallas kernels: 113 us -> 98.7 us
  local copies, waits for them, and re-layouts: 9.35 us -> 0 us
  other arithmetic: 6.47 us -> 0 us
    pallas_call x1, Pallas kernels: 113 us -> 96.4 us  [fused(): pl.pallas_call(kernel, out_shape=(jax.ShapeDtypeStruct((TOK, TOK, d), BF1...]
    unnamed x5 -> x0, local copies, waits for them, and re-layouts: 4.79 us -> none
    pallas_call x0 -> x1, Pallas kernels: none -> 2.34 us  [handed_over(): pl.pallas_call(hand_over, out_shape=tuple((jax.ShapeDtypeStruct(a.shape,...]
    select_n x2 -> x0, other arithmetic: 2.03 us -> none  [the longest x1 1.99 us: body(): new_bias = jnp.where(is_dead, 0.0, enc_bias[0])[None]]
    concatenate x1 -> x0, local copies, waits for them, and re-layouts: 1.74 us -> none  [body(): jnp.concatenate([residuals, (place // 64).astype(BF16), (place % 64).asty...]
    broadcast_in_dim x3 -> x0, local copies, waits for them, and re-layouts: 1.42 us -> none  [the longest x1 0.75 us: seed_positions(): return jnp.broadcast_to(pos[:, None], (pos.shape[0], 128))]
    unnamed x1 -> x0, other arithmetic: 1.34 us -> none
where the time goes in v3:
time: 99.7 us; the launch traced here: 99.5 us
  Pallas kernels  98.7 us (99%)
    pallas_call x1, Pallas kernels, fused(): pl.pallas_call(kernel, out_shape=(jax.ShapeDtypeStruct((TOK, TOK, d), BF1...  96.4 us
    pallas_call x1, Pallas kernels, handed_over(): pl.pallas_call(hand_over, out_shape=tuple((jax.ShapeDtypeStruct(a.shape,...  2.34 us

profile of v3, /device:TPU:0, one launch (start us, length us, event | category | flops | bytes accessed | tf_op | source)
XLA Modules:
  0.0 99.5 jit_solution(10637134788932127862)
XLA Ops:
  0.6 96.4 %sae.1 = (bf16[8,8,2048]{2,1,0:T(8,128)(2,1)}, f32[1]{0:T(128)}, f32[32,128]{1,0:T(8,128)}, bf16[16,2048]{1,0:T(8,128)(2,1)}, f32[32,128]{1,0:T(8,128)}) custom-call(bf16[8,8,2048]{2,1,0:T(8,128)(2,1)} %res.1, s32[8,8,64]{2,1,0:T(8,128)} %slots.1, bf16[4096,2048]{1,0:T(8,128)(2,1)} %bitcast.5, f32[1,2048]{1,0:T(1,128)} %dec.1, f32[32,128]{1,0:T(8,128)} %bitcast.6, ...), custom_call_target="tpu_custom_call" | custom-call | tf_op jit(solution)/shard_map/sae/pallas_call | solution.py:570
  97.0 2.3 %hand_over.1 = (f32[1]{0:T(128)}, bf16[8,8,2048]{2,1,0:T(8,128)(2,1)}, f32[32,128]{1,0:T(8,128)}, bf16[16,2048]{1,0:T(8,128)(2,1)}, f32[32,128]{1,0:T(8,128)}) custom-call(f32[1]{0:T(128)} %get-tuple-element.15.refs_0_, bf16[8,8,2048]{2,1,0:T(8,128)(2,1)} %get-tuple-element.16.refs_1_, f32[32,128]{1,0:T(8,128)} %get-tuple-element.17.refs_2_, ...), custom_call_target="tpu_custom_call" | custom-call | tf_op jit(solution)/shard_map/hand_over/pallas_call | solution.py:518

commit v4 on v3

--- a/solution.py
+++ b/solution.py
@@ -16,7 +16,7 @@
 BF16 = jnp.bfloat16
 TILE = 1024
 STAT = 512
-COLS = 1024
+COLS = 2048
 TOK = 8
 HALF = 32
 BLOCK = 256
@@ -73,7 +73,7 @@
     for j in range(1, tiles):
         product(j)
         activity(j - 1)
-        if j == 1:
+        if j == 3:
             between()
     activity(tiles - 1)
 
@@ -232,7 +232,9 @@
         for dx, dz in plane
     ]
     start(square_copies)
-    stats(1)
+    for q in (1, 2, 3):
+        stats(q)
+    places[...] = seed_places(seed_tokens, x, z)
     arrive(first)
 
     def beside(h):
@@ -251,9 +253,6 @@
     beside_a, beside_b = beside(0), beside(1)
     start(beside_a)
     sent.extend(across + beside_b)
-    stats(2)
-    stats(3)
-    places[...] = seed_places(seed_tokens, x, z)
     arrive(square_copies)
     scale = lax.rsqrt(jnp.sum(squares[...], axis=0)[0:1, 0:1] / (tokens * d))
 
@@ -361,10 +360,10 @@
 
     hot = one_hot(places[...], tokens)
 
-    @pl.loop(0, d // 512)
+    @pl.loop(0, d // 1024)
     def _(n):
-        at = pl.ds(pl.multiple_of(n * 512, 512), 512)
-        others = part[1:, :, at].reshape(3 * BLOCK, 512)
+        at = pl.ds(pl.multiple_of(n * 1024, 1024), 1024)
+        others = part[1:, :, at].reshape(3 * BLOCK, 1024)
         picked[:, at] = jnp.dot(hot[:, BLOCK:], others, preferred_element_type=F32)
 
     decode(0, coef.at[0])
@@ -388,11 +387,11 @@
     arrive(near_a)
     last = [combine(0)]
 
-    @pl.loop(0, d // 512)
+    @pl.loop(0, d // 1024)
     def _(n):
-        at = pl.ds(pl.multiple_of(n * 512, 512), 512)
+        at = pl.ds(pl.multiple_of(n * 1024, 1024), 1024)
         v = jnp.dot(hot[:, :BLOCK], part[0, :, at], preferred_element_type=F32) + picked[:, at]
-        seeds[:, :, :, :, at] = v.reshape(4, 2, 4, RES, 512).astype(BF16)
+        seeds[:, :, :, :, at] = v.reshape(4, 2, 4, RES, 1024).astype(BF16)
 
     seed_copies = []
     for k in (2, 1, 3):

time: 99.7 us -> 96.5 us (0.968)
  Pallas kernels: 98.7 us -> 95.4 us
    pallas_call x1, Pallas kernels: 96.4 us -> 93.1 us  [fused(): pl.pallas_call(kernel, out_shape=(jax.ShapeDtypeStruct((TOK, TOK, d), BF1...]
where the time goes in v4:
time: 96.5 us; the launch traced here: 96.2 us
  Pallas kernels  95.4 us (99%)
    pallas_call x1, Pallas kernels, fused(): pl.pallas_call(kernel, out_shape=(jax.ShapeDtypeStruct((TOK, TOK, d), BF1...  93.1 us
    pallas_call x1, Pallas kernels, handed_over(): pl.pallas_call(hand_over, out_shape=tuple((jax.ShapeDtypeStruct(a.shape,...  2.34 us

profile of v4, /device:TPU:0, one launch (start us, length us, event | category | flops | bytes accessed | tf_op | source)
XLA Modules:
  0.0 96.2 jit_solution(14626241439063250994)
XLA Ops:
  0.6 93.1 %sae.1 = (bf16[8,8,2048]{2,1,0:T(8,128)(2,1)}, f32[1]{0:T(128)}, f32[32,128]{1,0:T(8,128)}, bf16[16,2048]{1,0:T(8,128)(2,1)}, f32[32,128]{1,0:T(8,128)}) custom-call(bf16[8,8,2048]{2,1,0:T(8,128)(2,1)} %res.1, s32[8,8,64]{2,1,0:T(8,128)} %slots.1, bf16[4096,2048]{1,0:T(8,128)(2,1)} %bitcast.5, f32[1,2048]{1,0:T(1,128)} %dec.1, f32[32,128]{1,0:T(8,128)} %bitcast.6, ...), custom_call_target="tpu_custom_call" | custom-call | tf_op jit(solution)/shard_map/sae/pallas_call | solution.py:569
  93.7 2.3 %hand_over.1 = (f32[1]{0:T(128)}, bf16[8,8,2048]{2,1,0:T(8,128)(2,1)}, f32[32,128]{1,0:T(8,128)}, bf16[16,2048]{1,0:T(8,128)(2,1)}, f32[32,128]{1,0:T(8,128)}) custom-call(f32[1]{0:T(128)} %get-tuple-element.15.refs_0_, bf16[8,8,2048]{2,1,0:T(8,128)(2,1)} %get-tuple-element.16.refs_1_, f32[32,128]{1,0:T(8,128)} %get-tuple-element.17.refs_2_, ...), custom_call_target="tpu_custom_call" | custom-call | tf_op jit(solution)/shard_map/hand_over/pallas_call | solution.py:517

commit v5 on v4

--- a/solution.py
+++ b/solution.py
@@ -332,18 +332,13 @@
         mine = jnp.minimum(step, 1)
         encode(nf.at[step], w, bits, inv, bias, mass, coef.at[mine], p, between)
 
+        @pl.when(step > 0)
+        def _():
+            decode(step, coef.at[1])
+
         @pl.when(step == 1)
         def _():
-            for copy in beside_b:
-                copy.start()
-
-        @pl.when(step > 0)
-        def _():
-            decode(step, coef.at[1])
-
-        @pl.when(step == 1)
-        def _():
-            for copy in near_a:
+            for copy in beside_b + near_a:
                 copy.start()
 
         @pl.when(step == 2)

time: 96.5 us -> 95.9 us (level)
  no operation moved by 1% of the time
where the time goes in v5:
time: 95.9 us; the launch traced here: 95.6 us
  Pallas kernels  94.8 us (99%)
    pallas_call x1, Pallas kernels, fused(): pl.pallas_call(kernel, out_shape=(jax.ShapeDtypeStruct((TOK, TOK, d), BF1...  92.5 us
    pallas_call x1, Pallas kernels, handed_over(): pl.pallas_call(hand_over, out_shape=tuple((jax.ShapeDtypeStruct(a.shape,...  2.34 us

profile of v5, /device:TPU:0, one launch (start us, length us, event | category | flops | bytes accessed | tf_op | source)
XLA Modules:
  0.0 95.6 jit_solution(17227625104340720844)
XLA Ops:
  0.6 92.5 %sae.1 = (bf16[8,8,2048]{2,1,0:T(8,128)(2,1)}, f32[1]{0:T(128)}, f32[32,128]{1,0:T(8,128)}, bf16[16,2048]{1,0:T(8,128)(2,1)}, f32[32,128]{1,0:T(8,128)}) custom-call(bf16[8,8,2048]{2,1,0:T(8,128)(2,1)} %res.1, s32[8,8,64]{2,1,0:T(8,128)} %slots.1, bf16[4096,2048]{1,0:T(8,128)(2,1)} %bitcast.5, f32[1,2048]{1,0:T(1,128)} %dec.1, f32[32,128]{1,0:T(8,128)} %bitcast.6, ...), custom_call_target="tpu_custom_call" | custom-call | tf_op jit(solution)/shard_map/sae/pallas_call | solution.py:564
  93.1 2.3 %hand_over.1 = (f32[1]{0:T(128)}, bf16[8,8,2048]{2,1,0:T(8,128)(2,1)}, f32[32,128]{1,0:T(8,128)}, bf16[16,2048]{1,0:T(8,128)(2,1)}, f32[32,128]{1,0:T(8,128)}) custom-call(f32[1]{0:T(128)} %get-tuple-element.15.refs_0_, bf16[8,8,2048]{2,1,0:T(8,128)(2,1)} %get-tuple-element.16.refs_1_, f32[32,128]{1,0:T(8,128)} %get-tuple-element.17.refs_2_, ...), custom_call_target="tpu_custom_call" | custom-call | tf_op jit(solution)/shard_map/hand_over/pallas_call | solution.py:512
